TPU v7x, 32 devices: a whole 2x2x4 slice. The times are simulated.
32 devices in a mesh: lat: 16 (over z, y, x), lon: 2 (over core).
Axes of the slice: x: 2, y: 2, z: 4, core: 2. Of those that a mesh axis runs over, the one named last changes fastest.
Arguments:
- elevation: float32 [1, 3072, 8640], P(None, 'lat', 'lon'), may hold values from -30 to 30
- velocity: float32 [1, 2, 3072, 8640], P(None, None, 'lat', 'lon'), may hold values from -3 to 3
- wind_forcing: float32 [2, 3072, 8640], P(None, 'lat', 'lon'), may hold values from -0.6 to 0.6
- ocean_depth: float32 [3072, 8640], P('lat', 'lon'), may hold values from 0.2 to 1
- wet_mask: int32 [3072, 8640], P('lat', 'lon'), may hold values from 0 to 1, as said below
- love_factor: float32 [1081], replicated, may hold values from 0.3 to 3
- wavenumbers: int32 [16], replicated, may hold values from 0 to 31, as said below
Outputs:
- new_elevation: float32 [1, 3072, 8640], P(None, 'lat', 'lon')
- new_velocity: float32 [1, 2, 3072, 8640], P(None, None, 'lat', 'lon')
- self_loading: float32 [1, 3072, 8640], P(None, 'lat', 'lon')
Inputs may be any that keep to these rules, and one draw needn't show every extreme that they name: `wet_mask`: 0 in the 24 rows nearest each pole. `wavenumbers`: distinct.
All inputs are finite; a program needn't handle non-finite values.
Results may differ from a plain program's by a relative error of at most 0.0003.
Values sent between devices are 32-bit elements; how exact they have to be, the bound alone decides.
No kernel may reach another device: no remote copies, remote signals or barrier semaphores. Data moves between devices by JAX's collectives and lax.ppermute only.
A program may use at most 128 MiB of HBM per device.

v0:
```python
import math

import jax
import jax.numpy as jnp
from jax import lax
from jax.experimental import pallas as pl
from jax.experimental.pallas import tpu as pltpu
from jax.sharding import PartitionSpec as P

GRID_LAT = 3072
GRID_LON = 8640
DEGREES = 1081
LANES = 128

f32 = jnp.float32
bf16 = jnp.bfloat16
SMEM = pl.BlockSpec(memory_space=pltpu.SMEM)
VMEM = pl.BlockSpec(memory_space=pltpu.VMEM)
ANY = pl.BlockSpec(memory_space=pl.ANY)
HBM = pl.BlockSpec(memory_space=pltpu.HBM)
NT = (((1,), (1,)), ((), ()))
TN = (((0,), (0,)), ((), ()))


def round_up(value, step):
    return -(-value // step) * step


def sine_series(angle, orders=(13, 11, 9, 7, 5, 3, 1)):
    square = angle * angle
    series = None
    for order in orders:
        factor = (-1.0 if (order // 2) % 2 else 1.0) / math.factorial(order)
        series = jnp.full(angle.shape, factor, f32) if series is None else series * square + factor
    return angle * series


def cosine_of_units(units):
    turns = jnp.floor(units * (1.0 / GRID_LON) + 0.5)
    sine = sine_series((units - turns * GRID_LON) * (math.pi / GRID_LON))
    return 1.0 - 2.0 * sine * sine


def colatitude(row):
    return jnp.pi * (row.astype(f32) + 0.5) / GRID_LAT


def sine_of(angle):
    return sine_series(angle, (15, 13, 11, 9, 7, 5, 3, 1))


def split(value):
    high = value.astype(bf16)
    return high, (value - high.astype(f32)).astype(bf16)


def edge_kernel(rows, cols, width, lat, lon, waves, lane_rows):
    tail = cols % LANES or LANES

    def body(band_ref, sector_ref, waves_ref, elev, vel, wind, depth, wet,
             send, top, bottom, side, table, elev_v, wet_v, load_hi, load_lo,
             top_v, bottom_v, left_v, right_v, sems):
        band = band_ref[0]
        sector = sector_ref[0]
        first = pltpu.make_async_copy(elev.at[0], elev_v, sems.at[0])
        second = pltpu.make_async_copy(wet, wet_v, sems.at[1])
        first.start()
        second.start()
        fields = (vel.at[0, 0], vel.at[0, 1], wind.at[1], depth)
        copies = []
        for n, field in enumerate(fields):
            copies.append(pltpu.make_async_copy(field.at[pl.ds(0, 1), :], top_v.at[n], sems.at[2 + n]))
            copies.append(pltpu.make_async_copy(field.at[pl.ds(rows - 1, 1), :], bottom_v.at[n], sems.at[6 + n]))
        fields = (vel.at[0, 0], vel.at[0, 1], wind.at[0], depth)
        for n, field in enumerate(fields):
            copies.append(pltpu.make_async_copy(field.at[:, pl.ds(0, LANES)], left_v.at[n], sems.at[10 + n]))
            copies.append(pltpu.make_async_copy(
                field.at[:, pl.ds(cols - tail, tail)], right_v.at[n], sems.at[14 + n]))
        for copy in copies:
            copy.start()

        wave_row = lax.broadcasted_iota(jnp.int32, (2 * waves, LANES), 0)
        order = jnp.zeros((2 * waves, LANES), f32)
        for n in range(waves):
            order = jnp.where(wave_row // 2 == n, waves_ref[n].astype(f32), order)
        quarter = jnp.where(wave_row % 2 == 1, 0.25 * GRID_LON, 0.0)
        lane = lax.broadcasted_iota(jnp.int32, (2 * waves, LANES), 1)
        for tile in range(width // LANES):
            column = (sector * cols + (tile - 1) * LANES + lane).astype(f32)
            values = cosine_of_units(order * column - quarter)
            high, low = split(values)
            span = slice(tile * LANES, (tile + 1) * LANES)
            table[0 : 2 * waves, span] = high
            table[2 * waves : 4 * waves, span] = high
            table[4 * waves : 6 * waves, span] = low

        first.wait()
        second.wait()
        for start in range(0, rows, 8):
            here = slice(start, start + 8)
            high, low = split(elev_v[here, :] * wet_v[here, :].astype(f32))
            load_hi[here, :] = high
            load_lo[here, :] = low
        own = slice(LANES, LANES + cols)
        main_part = lax.dot_general(
            load_hi[...], table[2 * waves : 6 * waves, own], NT, preferred_element_type=f32)
        rest = lax.dot_general(load_lo[...], table[0 : 2 * waves, own], NT, preferred_element_type=f32)
        sums = (main_part[:, 0 : 2 * waves] + main_part[:, 2 * waves : 4 * waves] + rest) * (1.0 / GRID_LON)
        row = lax.broadcasted_iota(jnp.int32, (rows, lane_rows), 0)
        slot = lax.broadcasted_iota(jnp.int32, (rows, lane_rows), 1) - 2
        target = jnp.where(band < lat // 2, row, rows - 1 - row)
        pick = jnp.where(slot == target, 1.0, 0.0).astype(bf16)
        high, low = split(sums)
        lower = (sums - high.astype(f32) - low.astype(f32)).astype(bf16)
        turned = (
            lax.dot_general(high, pick, TN, preferred_element_type=f32)
            + lax.dot_general(low, pick, TN, preferred_element_type=f32)
            + lax.dot_general(lower, pick, TN, preferred_element_type=f32)
        )
        for n in range(waves):
            block = turned[2 * n : 2 * n + 2, :]
            for k in range(lon):
                send[n * lon + k, :, :] = block

        for copy in copies:
            copy.wait()
        top[0:2, :] = elev_v[0:2, :]
        bottom[0:2, :] = elev_v[rows - 2 : rows, :]
        for n in range(4):
            top[2 + n : 3 + n, :] = top_v[n]
            bottom[2 + n : 3 + n, :] = bottom_v[n]
        top[6:7, :] = wet_v[0:1, :].astype(f32)
        bottom[6:7, :] = wet_v[rows - 1 : rows, :].astype(f32)
        top[7:8, :] = jnp.zeros((1, cols), f32)
        bottom[7:8, :] = jnp.zeros((1, cols), f32)
        blank = jnp.zeros((8, LANES - tail), f32)
        for start in range(0, rows, 8):
            here = slice(start, start + 8)
            lane8 = lax.broadcasted_iota(jnp.int32, (8, LANES), 1)
            left = [elev_v[here, 0:LANES]] + [left_v[n, here, :] for n in range(4)]
            left.append(wet_v[here, 0:LANES].astype(f32))
            right = [elev_v[here, cols - tail : cols]] + [right_v[n, here, :] for n in range(4)]
            right.append(wet_v[here, cols - tail : cols].astype(f32))
            right = [jnp.concatenate([x, blank], axis=1) if tail < LANES else x for x in right]
            packed = jnp.zeros((8, LANES), f32)
            for n in range(6):
                moved = pltpu.roll(left[n], 4 * n, 1) if n else left[n]
                packed = jnp.where(lane8 // 2 == 2 * n, moved, packed)
                moved = pltpu.roll(right[n], (4 * n + 2 - (tail - 2)) % LANES, 1)
                packed = jnp.where(lane8 // 2 == 2 * n + 1, moved, packed)
            side[here, :] = packed

    return pl.pallas_call(
        body,
        out_shape=(
            jax.ShapeDtypeStruct((lat * lon, 2, lane_rows), f32),
            jax.ShapeDtypeStruct((8, cols), f32),
            jax.ShapeDtypeStruct((8, cols), f32),
            jax.ShapeDtypeStruct((rows, LANES), f32),
            jax.ShapeDtypeStruct((6 * waves, width), bf16),
        ),
        in_specs=[SMEM, SMEM, SMEM, ANY, ANY, ANY, ANY, ANY],
        out_specs=(VMEM, VMEM, VMEM, VMEM, VMEM),
        scratch_shapes=[
            pltpu.VMEM((rows, cols), f32),
            pltpu.VMEM((rows, cols), jnp.int32),
            pltpu.VMEM((rows, cols), bf16),
            pltpu.VMEM((rows, cols), bf16),
            pltpu.VMEM((4, 1, cols), f32),
            pltpu.VMEM((4, 1, cols), f32),
            pltpu.VMEM((4, rows, LANES), f32),
            pltpu.VMEM((4, rows, tail), f32),
            pltpu.SemaphoreType.DMA((18,)),
        ],
        name="edge_fourier",
    )


GROW = 2.0**40
SHRINK = 2.0**-96
SHRINK_LOG = 96.0 * math.log(2.0)


def legendre_kernel(bands, rows, lane_rows, steps):
    tile = (8, LANES)
    spots = [(r, t) for r in range(0, bands, 8) for t in range(0, lane_rows, LANES)]
    pairs = 8
    parts = 4
    share = steps // parts

    def body(band_ref, sector_ref, waves_ref, values_out, coef_a, coef_s, coef_t, values, sems):
        order = waves_ref[band_ref[0]]
        parity = sector_ref[0] % 2
        order_real = order.astype(f32)
        count = coef_a.shape[0]
        for start in range(0, count, 8):
            index = (lax.broadcasted_iota(jnp.int32, tile, 0) + start).astype(f32)
            index = jnp.maximum(index, 1.0)
            double = 2.0 * (index + order_real)
            above = index + 2.0 * order_real
            below = double - 1.0
            raising = jnp.sqrt(below * (double + 1.0) / (index * above))
            ratio = raising / below
            coef_a[start : start + 8, :] = raising
            coef_s[start : start + 8, :] = ratio * above
            coef_t[start : start + 8, :] = ratio * (index - 1.0)
        ladder_rows = round_up(DEGREES, 8 * LANES) // LANES
        ladder = (
            lax.broadcasted_iota(jnp.int32, (ladder_rows, LANES), 0) * LANES
            + lax.broadcasted_iota(jnp.int32, (ladder_rows, LANES), 1)
        ).astype(f32)
        used = (ladder >= 2.0) & (ladder <= order_real)
        safe = jnp.maximum(ladder, 1.0)
        total = jnp.sum(jnp.where(used, jnp.log((2.0 * safe + 1.0) / (2.0 * safe)), 0.0))
        total = 0.5 * (total + jnp.where(order > 0, math.log(3.0), 0.0))

        gap, level, now, slope = [], [], [], []
        for r, t in spots:
            row = (
                (lax.broadcasted_iota(jnp.int32, tile, 0) + r) * rows
                + lax.broadcasted_iota(jnp.int32, tile, 1) + (t - 2)
            )
            angle = colatitude(jnp.clip(row, 0, GRID_LAT // 2 + 1))
            half = sine_series(0.5 * angle)
            cosine = 1.0 - 2.0 * half * half
            gap.append(1.0 - cosine)
            log_start = total + order_real * jnp.log(sine_of(angle))
            rung = jnp.minimum(jnp.ceil((log_start - math.log(GROW)) / SHRINK_LOG), 0.0)
            level.append(rung)
            now.append(jnp.exp(log_start - rung * SHRINK_LOG))
            slope.append(jnp.zeros(tile, f32))

        def scale_of(level):
            return jnp.where(level == 0.0, 1.0, jnp.where(level == -1.0, SHRINK, 0.0))

        def advance(k, now, slope):
            a = jnp.broadcast_to(coef_a[pl.ds(k, 1), :], tile)
            s = jnp.broadcast_to(coef_s[pl.ds(k, 1), :], tile)
            t = jnp.broadcast_to(coef_t[pl.ds(k, 1), :], tile)
            drop = [a * h for h in gap]
            kept = [t * y for y in slope]
            slope = [y - c * x for x, y, c in zip(now, kept, drop)]
            return [(s - c) * x + y for x, y, c in zip(now, kept, drop)], slope

        odd = parity == 1
        next_now, next_slope = advance(1, now, slope)
        now = [jnp.where(odd, y, x) for x, y in zip(now, next_now)]
        slope = [jnp.where(odd, y, x) for x, y in zip(slope, next_slope)]

        def block(n, carry):
            now, slope, level = carry
            scale = [scale_of(x) for x in level]
            for q in range(pairs):
                j = n * pairs + q
                for (r, t), x, y in zip(spots, now, scale):
                    values[pl.ds(j, 1), r : r + 8, t : t + LANES] = (x * y)[None]
                k = 2 * j + parity + 1
                now, slope = advance(k, now, slope)
                now, slope = advance(k + 1, now, slope)
            large = [(jnp.maximum(jnp.abs(x), jnp.abs(y)) > GROW) & (z < 0.0)
                     for x, y, z in zip(now, slope, level)]
            factor = [jnp.where(x, SHRINK, 1.0) for x in large]
            level = [jnp.where(x, z + 1.0, z) for x, z in zip(large, level)]
            return [x * y for x, y in zip(now, factor)], [x * y for x, y in zip(slope, factor)], level

        state = (now, slope, level)
        copies = []
        for k in range(parts):
            state = lax.fori_loop(k * share // pairs, (k + 1) * share // pairs, block, state)
            here = pl.ds(k * share, share)
            copies.append(pltpu.make_async_copy(values.at[here], values_out.at[here], sems.at[k]))
            copies[k].start()
        for copy in copies:
            copy.wait()

    coefs = pltpu.VMEM((2 * steps + 8, LANES), f32)
    return pl.pallas_call(
        body,
        out_shape=pltpu.HBM((steps, bands, lane_rows), f32),
        in_specs=[SMEM, SMEM, SMEM],
        out_specs=HBM,
        scratch_shapes=[coefs, coefs, coefs, pltpu.VMEM((steps, bands, lane_rows), f32),
                        pltpu.SemaphoreType.DMA((parts,))],
        compiler_params=pltpu.CompilerParams(vmem_limit_bytes=16 << 20),
        cost_estimate=pl.CostEstimate(flops=12 * steps * bands * lane_rows, transcendentals=0,
                                      bytes_accessed=4 * steps * bands * lane_rows),
        name="legendre_values",
    )


def synthesis_kernel(bands, rows, lane_rows, steps, lat, lon):
    parts = 4
    share = steps // parts

    def body(band_ref, sector_ref, waves_ref, love, got, values_in, send, mass, totals, values, sems):
        copies = []
        for k in range(parts):
            here = pl.ds(k * share, share)
            copies.append(pltpu.make_async_copy(values_in.at[here], values.at[here], sems.at[k]))
            copies[k].start()
        order = waves_ref[band_ref[0]]
        parity = sector_ref[0] % 2
        sign = jnp.where(parity == 1, -1.0, 1.0)
        slot = lax.broadcasted_iota(jnp.int32, (1, lane_rows), 1)
        inside = (slot >= 2) & (slot < rows + 2)
        for b in range(bands):
            north = got[b * lon]
            south = got[(lat - 1 - b) * lon]
            for k in range(1, lon):
                north = north + got[b * lon + k]
                south = south + got[(lat - 1 - b) * lon + k]
            row = b * rows + slot - 2
            sine = sine_of(colatitude(jnp.clip(row, 0, GRID_LAT // 2 + 1)))
            weight = (jnp.pi / (2.0 * GRID_LAT)) * sine
            both = jnp.where(inside, (north + sign * south) * weight, 0.0)
            mass[0, b : b + 1, :] = both[0:1]
            mass[1, b : b + 1, :] = both[1:2]
        sub = lax.broadcasted_iota(jnp.int32, (8, LANES), 0)
        tiles = [(r, t) for r in range(0, bands, 8) for t in range(0, lane_rows, LANES)]

        def fold(parts, shift):
            half = len(parts) // 2
            lower = sub % (2 * shift) < shift
            out = []
            for x, y in zip(parts[:half], parts[half:]):
                out.append(jnp.where(lower, y + pltpu.roll(y, 8 - shift, 0), x + pltpu.roll(x, shift, 0)))
            return out

        def analyse(n, carry):
            for c in range(2):
                parts = []
                for q in (7, 6, 5, 4, 3, 2, 1, 0):
                    acc = None
                    for r, t in tiles:
                        term = mass[c, r : r + 8, t : t + LANES] * values[n * 8 + q, r : r + 8, t : t + LANES]
                        acc = term if acc is None else acc + term
                    parts.append(acc)
                for shift in (4, 2, 1):
                    parts = fold(parts, shift)
                totals[c, pl.ds(n * 8, 8), :] = parts[0]
            return carry

        for k in range(parts):
            copies[k].wait()
            lax.fori_loop(k * share // 8, (k + 1) * share // 8, analyse, 0)
        degree = order + parity + 2 * lax.broadcasted_iota(jnp.int32, (steps, LANES), 0)
        weight = jnp.where(degree < DEGREES, 1.0 / (2.0 * degree.astype(f32) + 1.0), 0.0)
        for c in range(2):
            totals[c] = jnp.sum(totals[c], axis=1, keepdims=True) * weight

        def synthesise(n, carry):
            carry = list(carry)
            for q in range(8):
                j = n * 8 + q
                weight = love[jnp.minimum(order + parity + 2 * j, DEGREES - 1)]
                factors = [jnp.broadcast_to(totals[c, pl.ds(j, 1), :], (8, LANES)) * weight for c in range(2)]
                for i, (r, t) in enumerate(tiles):
                    value = values[j, r : r + 8, t : t + LANES]
                    for c in range(2):
                        carry[2 * i + c] = carry[2 * i + c] + factors[c] * value
            return tuple(carry)

        zero = jnp.zeros((8, LANES), f32)
        found = lax.fori_loop(0, steps // 8, synthesise, (zero,) * (2 * len(tiles)))
        for b in range(bands):
            for t in range(0, lane_rows, LANES):
                i = tiles.index((b // 8 * 8, t))
                for c in range(2):
                    line = found[2 * i + c][b % 8 : b % 8 + 1, :]
                    for k in range(lon):
                        send[b * lon + k, c : c + 1, t : t + LANES] = line
                        send[(lat - 1 - b) * lon + k, c : c + 1, t : t + LANES] = line

    return pl.pallas_call(
        body,
        out_shape=jax.ShapeDtypeStruct((lat * lon, 2, lane_rows), f32),
        in_specs=[SMEM, SMEM, SMEM, SMEM, VMEM, HBM],
        out_specs=VMEM,
        scratch_shapes=[
            pltpu.VMEM((2, bands, lane_rows), f32),
            pltpu.VMEM((2, steps, LANES), f32),
            pltpu.VMEM((steps, bands, lane_rows), f32),
            pltpu.SemaphoreType.DMA((parts,)),
        ],
        compiler_params=pltpu.CompilerParams(vmem_limit_bytes=16 << 20),
        name="degree_sums",
    )


def step_kernel(rows, cols, width, lat, waves, lane_rows):
    tail = cols % LANES or LANES
    tiles = -(-cols // LANES)
    tall = rows + 32
    top = 16
    own = slice(LANES, LANES + cols)
    meridional = 0.1 * GRID_LAT / GRID_LON
    pieces = 6 if rows % 96 == 0 else 1
    piece = rows // pieces
    names = 6

    def body(band_ref, sector_ref, got, table, low, high, low_side, high_side,
             elev, vel, wind, depth, wet, elev_out, vel_out, load_out,
             elev_v, u_v, v_v, wx_v, wy_v, depth_v, wet_v, surf, flux, load_v,
             left_v, right_v, zonal, sine_v, merid, sems, out_sems):
        band = band_ref[0]
        fields = (
            (elev.at[0], elev_v), (depth, depth_v), (wet, wet_v), (vel.at[0, 0], u_v),
            (vel.at[0, 1], v_v), (wind.at[1], wy_v), (wind.at[0], wx_v),
        )
        copies = []
        for k in range(pieces):
            inside = pl.ds(top + k * piece, piece)
            outside = pl.ds(k * piece, piece)
            copies.append([pltpu.make_async_copy(
                source.at[outside, :], buffer.at[inside, :], sems.at[k, n])
                for n, (source, buffer) in enumerate(fields)])
            for copy in copies[k]:
                copy.start()

        row = lax.broadcasted_iota(jnp.int32, (tall, LANES), 0) - top + band * rows
        row = jnp.clip(row, 0, GRID_LAT - 1)
        sine = sine_of(colatitude(jnp.minimum(row, GRID_LAT - 1 - row)))
        sine_v[...] = sine
        zonal[...] = 0.05 / sine
        merid[...] = meridional / sine

        sign = jnp.where(band < lat // 2, 1.0, -1.0)
        mixed = (got[:, 0] + sign * got[:, 1]).reshape(2 * waves, lane_rows)
        first, second = split(mixed)
        stacked = jnp.concatenate([first, second, first], axis=0)
        line = lax.broadcasted_iota(jnp.int32, (rows + 8, lane_rows), 0)
        line = jnp.where(line < rows, line, jnp.where(line < rows + 2, line - rows - 2, line - 2))
        slot = lax.broadcasted_iota(jnp.int32, (rows + 8, lane_rows), 1)
        target = jnp.where(band < lat // 2, line + 2, rows + 1 - line)
        pick = jnp.where(slot == target, 1.0, 0.0).astype(bf16)
        factors = lax.dot_general(pick, stacked, NT, preferred_element_type=f32).astype(bf16)

        here = slice(top, top + rows)
        for n in range(names):
            left_v[n, here, :] = pltpu.roll(low_side[...], (124 - 4 * n) % LANES, 1)
            right_v[n, here, :] = pltpu.roll(high_side[...], (tail - 4 * n) % LANES, 1)

        elev_v[top - 2 : top, :] = low[0:2, :]
        elev_v[top + rows : top + rows + 2, :] = high[0:2, :]
        for n, buffer in enumerate((u_v, v_v, wy_v, depth_v, wet_v)):
            buffer[top - 1 : top, :] = low[2 + n : 3 + n, :].astype(buffer.dtype)
            buffer[top + rows : top + rows + 1, :] = high[2 + n : 3 + n, :].astype(buffer.dtype)

        group = 4
        after = slice(top + rows, top + rows + 2)
        for t in range(0, width // LANES, group):
            begin = t * LANES
            end = min((t + group) * LANES, width)
            loading = lax.dot_general(
                factors, table[:, begin:end], (((1,), (0,)), ((), ())), preferred_element_type=f32)
            surf[here, begin:end] = loading[0:rows]
            first_lane = max(begin, LANES)
            last_lane = min(end, LANES + cols)
            inner = slice(first_lane - LANES, last_lane - LANES)
            outer = slice(first_lane, last_lane)
            cut = slice(first_lane - begin, last_lane - begin)
            load_v[:, inner] = loading[0:rows, cut]
            surf[top - 2 : top, outer] = elev_v[top - 2 : top, inner] - loading[rows : rows + 2, cut]
            surf[after, outer] = elev_v[after, inner] - loading[rows + 2 : rows + 4, cut]
        load_copy = pltpu.make_async_copy(load_v, load_out.at[0], out_sems.at[0])
        load_copy.start()

        lane8 = lax.broadcasted_iota(jnp.int32, (8, LANES), 1)
        sub8 = lax.broadcasted_iota(jnp.int32, (8, LANES), 0)
        count = width // LANES

        def part(t):
            return slice(t * LANES, (t + 1) * LANES)

        def fetch(t, rows8, n, buffer):
            if t == 0:
                return left_v[n, rows8, :]
            if t <= cols // LANES:
                return buffer[rows8, part(t - 1)].astype(f32)
            if tail == LANES:
                return right_v[n, rows8, :]
            return jnp.concatenate(
                [buffer[rows8, cols - tail : cols].astype(f32), right_v[n, rows8, tail:LANES]], axis=1)

        def keep(buffer, rows8, t, value):
            if 0 < t <= cols // LANES:
                buffer[rows8, part(t - 1)] = value
            elif t and tail < LANES:
                buffer[rows8, cols - tail : cols] = value[:, 0:tail]

        def surfaces(n, carry):
            rows8 = pl.ds(pl.multiple_of(n * 8, 8), 8)
            for t in range(count):
                surf[rows8, part(t)] = fetch(t, rows8, 0, elev_v) - surf[rows8, part(t)]
            return carry

        def vertical(ref, base, at, centre):
            before = jnp.where(sub8 == 7, ref[pl.ds(base - 8, 8), at], centre)
            after = jnp.where(sub8 == 0, ref[pl.ds(base + 8, 8), at], centre)
            return pltpu.roll(after, 7, 0) - pltpu.roll(before, 1, 0)

        def across(behind, centre, ahead):
            ahead = jnp.where(lane8 == 0, ahead, centre)
            behind = jnp.where(lane8 == LANES - 1, behind, centre)
            return pltpu.roll(ahead, LANES - 1, 1) - pltpu.roll(behind, 1, 1)

        def speeds(n):
            base = pl.multiple_of(n * 8, 8)
            rows8 = pl.ds(base, 8)
            zs = zonal[rows8, :]
            sn = sine_v[rows8, :]
            level = [surf[rows8, part(0)], surf[rows8, part(0)]]
            flow = []
            wet_before = None
            for t in range(count + 1):
                if t < count:
                    at = part(t)
                    level.append(surf[rows8, part(t + 1)] if t + 1 < count else level[-1])
                    level.pop(0) if len(level) > 3 else None
                    u = fetch(t, rows8, 1, u_v)
                    v = fetch(t, rows8, 2, v_v)
                    d = fetch(t, rows8, 4, depth_v)
                    wet = fetch(t, rows8, 5, wet_v)
                    drag = wet / (d + 0.1 * jnp.sqrt(u * u + v * v))
                    new_u = drag * (u * d + fetch(t, rows8, 3, wx_v) - (zs * d) * across(*level))
                    keep(wx_v, rows8, t, new_u)
                    flow.append(d * new_u)
                    if t and not (t > cols // LANES and tail == LANES):
                        if t <= cols // LANES:
                            push = wy_v[rows8, part(t - 1)]
                        else:
                            push = jnp.concatenate(
                                [wy_v[rows8, cols - tail : cols], jnp.zeros((8, LANES - tail), f32)], axis=1)
                        new_v = drag * (v * d + push - (meridional * d) * vertical(surf, base, at, level[1]))
                        keep(wy_v, rows8, t, new_v)
                        flux[rows8, at] = sn * d * new_v
                else:
                    flow.append(flow[-1])
                if len(flow) > 3:
                    flow.pop(0)
                back = t - 1
                if len(flow) == 3 and 0 < back <= tiles:
                    change = wet_before * (zs * across(*flow))
                    if back <= cols // LANES:
                        elev_v[rows8, part(back - 1)] = elev_v[rows8, part(back - 1)] - change
                    else:
                        elev_v[rows8, cols - tail : cols] = elev_v[rows8, cols - tail : cols] - change[:, 0:tail]
                wet_before = wet

        def levels(n):
            base = pl.multiple_of(n * 8, 8)
            rows8 = pl.ds(base, 8)
            ms = merid[rows8, :]
            for t in range(1, tiles + 1):
                change = ms * vertical(flux, base, part(t), flux[rows8, part(t)])
                if t <= cols // LANES:
                    at = part(t - 1)
                else:
                    at = slice(cols - tail, cols)
                    change = change[:, 0:tail]
                elev_v[rows8, at] = elev_v[rows8, at] - wet_v[rows8, at].astype(f32) * change

        def out_copies(k):
            inside = pl.ds(top + k * piece, piece)
            outside = pl.ds(k * piece, piece)
            return (
                pltpu.make_async_copy(wx_v.at[inside, :], vel_out.at[0, 0, outside, :], out_sems.at[1 + k]),
                pltpu.make_async_copy(wy_v.at[inside, :], vel_out.at[0, 1, outside, :], out_sems.at[1 + pieces + k]),
                pltpu.make_async_copy(elev_v.at[inside, :], elev_out.at[0, outside, :], out_sems.at[1 + 2 * pieces + k]),
            )

        def both(n, carry):
            speeds(n + 1)
            levels(n)
            return carry

        def ahead_rows(n, carry):
            speeds(n)
            return carry

        per = piece // 8
        begin = top // 8
        done = begin
        for k in range(pieces):
            for copy in copies[k]:
                copy.wait()
            lax.fori_loop(begin + k * per, begin + (k + 1) * per, surfaces, 0)
            if k == 0:
                lax.fori_loop(begin - 1, begin + 1, ahead_rows, 0)
            stop = begin + (k + 1) * per - (2 if k + 1 < pieces else 0)
            lax.fori_loop(done, stop, both, 0)
            done = stop
            if k:
                for copy in out_copies(k - 1):
                    copy.start()
        for copy in out_copies(pieces - 1):
            copy.start()
        for k in range(pieces):
            for copy in out_copies(k):
                copy.wait()
        load_copy.wait()

    flat = pltpu.VMEM((tall, cols), f32)
    big = pltpu.VMEM((tall, width), f32)
    thin = pltpu.VMEM((tall, LANES), f32)
    return pl.pallas_call(
        body,
        out_shape=(
            jax.ShapeDtypeStruct((1, rows, cols), f32),
            jax.ShapeDtypeStruct((1, 2, rows, cols), f32),
            jax.ShapeDtypeStruct((1, rows, cols), f32),
        ),
        in_specs=[SMEM, SMEM, VMEM, VMEM, VMEM, VMEM, VMEM, VMEM, ANY, ANY, ANY, ANY, ANY],
        out_specs=(ANY, ANY, ANY),
        scratch_shapes=[
            flat, flat, flat, flat, flat, flat, pltpu.VMEM((tall, cols), jnp.int32), big, big,
            pltpu.VMEM((rows, cols), f32),
            pltpu.VMEM((names, tall, LANES), f32),
            pltpu.VMEM((names, tall, LANES), f32),
            thin, thin, thin,
            pltpu.SemaphoreType.DMA((pieces, 7)),
            pltpu.SemaphoreType.DMA((1 + 3 * pieces,)),
        ],
        compiler_params=pltpu.CompilerParams(vmem_limit_bytes=52 << 20),
        name="surge_step",
    )


def local(elevation, velocity, wind_forcing, ocean_depth, wet_mask, love_factor, wavenumbers):
    members, rows, cols = elevation.shape
    lat = lax.axis_size("lat")
    lon = lax.axis_size("lon")
    waves = wavenumbers.shape[0]
    assert members == 1 and waves == lat and lat % 16 == 0 and lon % 2 == 0
    bands = lat // 2
    lane_rows = round_up(rows + 4, LANES)
    width = LANES + round_up(cols + 2, LANES)
    steps = round_up((DEGREES + 1) // 2, 8)
    place = (
        lax.axis_index("lat").astype(jnp.int32)[None],
        lax.axis_index("lon").astype(jnp.int32)[None],
    )

    send, top, bottom, side, table = edge_kernel(rows, cols, width, lat, lon, waves, lane_rows)(
        *place, wavenumbers, elevation, velocity, wind_forcing, ocean_depth, wet_mask)
    got = lax.all_to_all(send, ("lat", "lon"), split_axis=0, concat_axis=0, tiled=True)
    values = legendre_kernel(bands, rows, lane_rows, steps)(*place, wavenumbers)
    values, bottom, top, side = lax.optimization_barrier((values, bottom, top, side))
    up = [(i, (i + 1) % lat) for i in range(lat)]
    down = [(i, (i - 1) % lat) for i in range(lat)]
    low = lax.ppermute(bottom, "lat", up)
    high = lax.ppermute(top, "lat", down)
    low_side = lax.ppermute(side, "lon", [(i, (i + 1) % lon) for i in range(lon)])
    high_side = low_side if lon == 2 else lax.ppermute(
        side, "lon", [(i, (i - 1) % lon) for i in range(lon)])
    send = synthesis_kernel(bands, rows, lane_rows, steps, lat, lon)(
        *place, wavenumbers, love_factor, got, pltpu.with_memory_space_constraint(values, pltpu.HBM))
    got = lax.all_to_all(send, ("lat", "lon"), split_axis=0, concat_axis=0, tiled=True)
    got = got.reshape(lat, lon, 2, lane_rows)[:, :2]
    return step_kernel(rows, cols, width, lat, waves, lane_rows)(
        *place, got, table, low, high, low_side, high_side,
        elevation, velocity, wind_forcing, ocean_depth, wet_mask)


def solution(mesh):
    return jax.shard_map(
        local,
        mesh=mesh,
        in_specs=(
            P(None, "lat", "lon"),
            P(None, None, "lat", "lon"),
            P(None, "lat", "lon"),
            P("lat", "lon"),
            P("lat", "lon"),
            P(),
            P(),
        ),
        out_specs=(P(None, "lat", "lon"), P(None, None, "lat", "lon"), P(None, "lat", "lon")),
        check_vma=False,
    )
```

profile of v0, /device:TPU:0, one launch (start us, length us, event | category | flops | bytes accessed | tf_op | source)
XLA Modules:
  0.0 56.7 jit_solution(13867318373961802478)
XLA Ops:
  0.6 0.0 copy-start.2
  0.6 6.6 %edge_fourier.1 = (f32[32,2,256]{2,1,0:T(2,128)}, f32[8,4320]{1,0:T(8,128)}, f32[8,4320]{1,0:T(8,128)}, f32[192,128]{1,0:T(8,128)}, bf16[96,4480]{1,0:T(8,128)(2,1)}) custom-call(s32[1]{0:T(128)} %bitcast.band_ref, s32[1]{0:T(128)} %bitcast.1.sector_ref, s32[16]{0:T(128)} %waves_ref.5, f32[1,192,4320]{2,1,0:T(8,128)} %elev.3, f32[1,2,192,4320]{3,2,1,0:T(8,128)} %vel.3, ...), custom_call_target="tpu_custom_call" | custom-call | tf_op jit(solution)/shard_map/edge_fourier/pallas_call | solution.py:644
  7.3 0.0 copy-start.4
  7.3 0.0 copy-start.3
  7.3 0.0 copy-start.1
  7.3 7.3 %all-to-all-start = ((f32[32,2,256]{2,1,0:T(2,128)}), f32[32,2,256]{2,1,0:T(2,128)S(1)}, u32[]{:S(2)}, u32[]{:S(2)}) async-start(f32[32,2,256]{2,1,0:T(2,128)} %get-tuple-element.12), calls=%async_computation | async-start | bytes 131072 | tf_op jit(solution)/shard_map/all_to_all | solution.py:646
  14.6 0.0 copy-done.2
  14.6 5.5 %legendre_values.1.values_in = f32[544,8,256]{2,1,0:T(8,128)} custom-call(s32[1]{0:T(128)} %bitcast.band_ref, s32[1]{0:T(128)} %bitcast.1.sector_ref, s32[16]{0:T(128)S(1)} %copy-done.2), custom_call_target="tpu_custom_call" | custom-call | flops 13369344 | bytes 4456448 | tf_op jit(solution)/shard_map/legendre_values/pallas_call | solution.py:647
  20.1 0.0 copy-start.5
  20.1 0.0 copy-start
  20.2 0.0 copy-done.4
  20.2 1.8 %collective-permute-start = (f32[8,4320]{1,0:T(8,128)S(1)}, f32[8,4320]{1,0:T(8,128)S(1)}, u32[]{:S(2)}, u32[]{:S(2)}) collective-permute-start(f32[8,4320]{1,0:T(8,128)S(1)} %copy-done.4), channel_id=1, source_target_pairs={{0,2},{2,4},{4,6},{6,8},{8,10},{10,12},{12,14},{14,16},{16,18},{18... | collective-permute-start | bytes 414728 | tf_op jit(solution)/shard_map/ppermute | solution.py:651
  22.0 0.0 copy-done.3
  22.0 3.9 %collective-permute-start.1 = (f32[8,4320]{1,0:T(8,128)S(1)}, f32[8,4320]{1,0:T(8,128)S(1)}, u32[]{:S(2)}, u32[]{:S(2)}) collective-permute-start(f32[8,4320]{1,0:T(8,128)S(1)} %copy-done.3), channel_id=1, source_target_pairs={{0,30},{2,0},{4,2},{6,4},{8,6},{10,8},{12,10},{14,12},{16,14},{18,... | collective-permute-start | bytes 414728 | tf_op jit(solution)/shard_map/ppermute | solution.py:652
  25.8 0.0 all-to-all-done.got
  25.9 0.0 copy-done.1
  25.9 5.8 %degree_sums.1 = f32[32,2,256]{2,1,0:T(2,128)} custom-call(s32[1]{0:T(128)} %bitcast.band_ref, s32[1]{0:T(128)} %bitcast.1.sector_ref, s32[16]{0:T(128)S(1)} %copy-done.2, f32[1081]{0:T(1024)S(1)} %copy-done.1, f32[32,2,256]{2,1,0:T(2,128)S(1)} %all-to-all-done.got, f32[544,8,256]{2,1,0:T(8,128)} %legendre_values.1.values_in), custom_call_target="tpu_custom_call" | custom-call | tf_op jit(solution)/shard_map/degree_sums/pallas_call | solution.py:656
  31.6 2.6 %all-to-all-start.1 = ((f32[32,2,256]{2,1,0:T(2,128)}), f32[32,2,256]{2,1,0:T(2,128)S(1)}, u32[]{:S(2)}, u32[]{:S(2)}) async-start(f32[32,2,256]{2,1,0:T(2,128)} %degree_sums.1), calls=%async_computation.1 | async-start | bytes 131072 | tf_op jit(solution)/shard_map/all_to_all | solution.py:658
  34.2 0.0 copy-done.5
  34.2 0.2 collective-permute-start.2
  34.4 1.2 %collective-permute-done.2.low_side.high_side = f32[192,128]{1,0:T(8,128)S(1)} collective-permute-done((f32[192,128]{1,0:T(8,128)S(1)}, f32[192,128]{1,0:T(8,128)S(1)}, u32[]{:S(2)}, u32[]{:S(2)}) %collective-permute-start.2) | collective-permute-done | bytes 98336 | tf_op jit(solution)/shard_map/ppermute | solution.py:653
  35.6 0.0 collective-permute-done.low
  35.6 0.0 collective-permute-done.1.high
  35.6 6.0 %all-to-all-done.1 = f32[32,2,256]{2,1,0:T(2,128)S(1)} async-done(((f32[32,2,256]{2,1,0:T(2,128)}), f32[32,2,256]{2,1,0:T(2,128)S(1)}, u32[]{:S(2)}, u32[]{:S(2)}) %all-to-all-start.1) | async-done | bytes 65568 | tf_op jit(solution)/shard_map/all_to_all | solution.py:658
  41.6 0.0 copy-done
  41.6 15.1 %surge_step.1 = (f32[1,192,4320]{2,1,0:T(8,128)}, f32[1,2,192,4320]{3,2,1,0:T(8,128)}, f32[1,192,4320]{2,1,0:T(8,128)}) custom-call(s32[1]{0:T(128)} %bitcast.band_ref, s32[1]{0:T(128)} %bitcast.1.sector_ref, f32[16,2,2,256]{3,2,1,0:T(2,128)S(1)} %bitcast.3, bf16[96,4480]{1,0:T(8,128)(2,1)S(1)} %copy-done, f32[8,4320]{1,0:T(8,128)S(1)} %collective-permute-done.low, ...), custom_call_target="tpu_custom_call" | custom-call | tf_op jit(solution)/shard_map/surge_step/pallas_call | solution.py:660
Async XLA Ops:
  0.6 14.0 %copy-start.2 = (s32[16]{0:T(128)S(1)}, s32[16]{0:T(128)}, u32[]{:S(2)}) copy-start(s32[16]{0:T(128)} %waves_ref.5) | copy-start | bytes 196
  7.3 12.9 %copy-start.4 = (f32[8,4320]{1,0:T(8,128)S(1)}, f32[8,4320]{1,0:T(8,128)}, u32[]{:S(2)}) copy-start(f32[8,4320]{1,0:T(8,128)} %get-tuple-element.18) | copy-start | bytes 414724
  7.3 14.7 %copy-start.3 = (f32[8,4320]{1,0:T(8,128)S(1)}, f32[8,4320]{1,0:T(8,128)}, u32[]{:S(2)}) copy-start(f32[8,4320]{1,0:T(8,128)} %get-tuple-element.19) | copy-start | bytes 414724
  7.3 18.6 %copy-start.1 = (f32[1081]{0:T(1024)S(1)}, f32[1081]{0:T(1024)}, u32[]{:S(2)}) copy-start(f32[1081]{0:T(1024)} %love.1) | copy-start | bytes 12976
  7.3 18.6 %all-to-all-start = ((f32[32,2,256]{2,1,0:T(2,128)}), f32[32,2,256]{2,1,0:T(2,128)S(1)}, u32[]{:S(2)}, u32[]{:S(2)}) async-start(f32[32,2,256]{2,1,0:T(2,128)} %get-tuple-element.12), calls=%async_computation | async-start | bytes 131072 | tf_op jit(solution)/shard_map/all_to_all | solution.py:646
  20.1 14.1 %copy-start.5 = (f32[192,128]{1,0:T(8,128)S(1)}, f32[192,128]{1,0:T(8,128)}, u32[]{:S(2)}) copy-start(f32[192,128]{1,0:T(8,128)} %get-tuple-element.20) | copy-start | bytes 294916
  20.1 21.5 %copy-start = (bf16[96,4480]{1,0:T(8,128)(2,1)S(1)}, bf16[96,4480]{1,0:T(8,128)(2,1)}, u32[]{:S(2)}) copy-start(bf16[96,4480]{1,0:T(8,128)(2,1)} %get-tuple-element.17.table) | copy-start | bytes 2580484
  20.2 15.4 %collective-permute-start = (f32[8,4320]{1,0:T(8,128)S(1)}, f32[8,4320]{1,0:T(8,128)S(1)}, u32[]{:S(2)}, u32[]{:S(2)}) collective-permute-start(f32[8,4320]{1,0:T(8,128)S(1)} %copy-done.4), channel_id=1, source_target_pairs={{0,2},{2,4},{4,6},{6,8},{8,10},{10,12},{12,14},{14,16},{16,18},{18... | collective-permute-start | bytes 414728 | tf_op jit(solution)/shard_map/ppermute | solution.py:651
  22.0 13.6 %collective-permute-start.1 = (f32[8,4320]{1,0:T(8,128)S(1)}, f32[8,4320]{1,0:T(8,128)S(1)}, u32[]{:S(2)}, u32[]{:S(2)}) collective-permute-start(f32[8,4320]{1,0:T(8,128)S(1)} %copy-done.3), channel_id=1, source_target_pairs={{0,30},{2,0},{4,2},{6,4},{8,6},{10,8},{12,10},{14,12},{16,14},{18,... | collective-permute-start | bytes 414728 | tf_op jit(solution)/shard_map/ppermute | solution.py:652
  31.6 10.0 %all-to-all-start.1 = ((f32[32,2,256]{2,1,0:T(2,128)}), f32[32,2,256]{2,1,0:T(2,128)S(1)}, u32[]{:S(2)}, u32[]{:S(2)}) async-start(f32[32,2,256]{2,1,0:T(2,128)} %degree_sums.1), calls=%async_computation.1 | async-start | bytes 131072 | tf_op jit(solution)/shard_map/all_to_all | solution.py:658
  34.2 1.4 %collective-permute-start.2 = (f32[192,128]{1,0:T(8,128)S(1)}, f32[192,128]{1,0:T(8,128)S(1)}, u32[]{:S(2)}, u32[]{:S(2)}) collective-permute-start(f32[192,128]{1,0:T(8,128)S(1)} %copy-done.5), channel_id=1, source_target_pairs={{0,1},{1,0},{2,3},{3,2},{4,5},{5,4},{6,7},{7,6},{8,9},{9,8},{10,11... | collective-permute-start | bytes 294920 | tf_op jit(solution)/shard_map/ppermute | solution.py:653
where the time goes:
time: 56.9 us; the launch traced here: 56.7 us
  Pallas kernels  32.9 us (58%)
  starting transfers between devices  15.8 us (28%)
  waiting for transfers between devices  7.22 us (13%)
  between operations  0.75 us (1%)
    pallas_call x1, Pallas kernels, local(): step_kernel(rows, cols, width, lat, waves, lane_rows)  15.1 us
    all_to_all x2, starting transfers between devices, local(): lax.all_to_all(send, ('lat', 'lon'), split_axis=0, concat_axis=0, tiled=T...  9.92 us
    pallas_call x1, Pallas kernels, local(): edge_kernel(rows, cols, width, lat, lon, waves, lane_rows)  6.61 us
    all_to_all x2, waiting for transfers between devices, local(): lax.all_to_all(send, ('lat', 'lon'), split_axis=0, concat_axis=0, tiled=T...  6.03 us
    pallas_call x1, Pallas kernels, local(): synthesis_kernel(bands, rows, lane_rows, steps, lat, lon)  5.75 us
    pallas_call x1, Pallas kernels, local(): values = legendre_kernel(bands, rows, lane_rows, steps)(*place, wavenumbers)  5.49 us
    ppermute x1, starting transfers between devices, local(): high = lax.ppermute(top, 'lat', down)  3.85 us
    ppermute x1, starting transfers between devices, local(): low = lax.ppermute(bottom, 'lat', up)  1.82 us
  transfers between devices with their start and end apart: 5, of which 2 were waited for; matrix products, arithmetic and copies ran while one was open for 0% of the time, Pallas kernels for 20%

commit v1 on v0

--- a/solution.py
+++ b/solution.py
@@ -6,6 +6,7 @@
 from jax.experimental import pallas as pl
 from jax.experimental.pallas import tpu as pltpu
 from jax.sharding import PartitionSpec as P
+
 
 GRID_LAT = 3072
 GRID_LON = 8640
@@ -392,7 +393,6 @@
     tiles = -(-cols // LANES)
     tall = rows + 32
     top = 16
-    own = slice(LANES, LANES + cols)
     meridional = 0.1 * GRID_LAT / GRID_LON
     pieces = 6 if rows % 96 == 0 else 1
     piece = rows // pieces
@@ -443,8 +443,11 @@
         elev_v[top - 2 : top, :] = low[0:2, :]
         elev_v[top + rows : top + rows + 2, :] = high[0:2, :]
         for n, buffer in enumerate((u_v, v_v, wy_v, depth_v, wet_v)):
-            buffer[top - 1 : top, :] = low[2 + n : 3 + n, :].astype(buffer.dtype)
-            buffer[top + rows : top + rows + 1, :] = high[2 + n : 3 + n, :].astype(buffer.dtype)
+            before, behind = low[2 + n : 3 + n, :], high[2 + n : 3 + n, :]
+            if buffer is depth_v:
+                before, behind = jnp.maximum(before, 0.2), jnp.maximum(behind, 0.2)
+            buffer[top - 1 : top, :] = before.astype(buffer.dtype)
+            buffer[top + rows : top + rows + 1, :] = behind.astype(buffer.dtype)
 
         group = 4
         after = slice(top + rows, top + rows + 2)
@@ -645,17 +648,17 @@
         *place, wavenumbers, elevation, velocity, wind_forcing, ocean_depth, wet_mask)
     got = lax.all_to_all(send, ("lat", "lon"), split_axis=0, concat_axis=0, tiled=True)
     values = legendre_kernel(bands, rows, lane_rows, steps)(*place, wavenumbers)
-    values, bottom, top, side = lax.optimization_barrier((values, bottom, top, side))
-    up = [(i, (i + 1) % lat) for i in range(lat)]
-    down = [(i, (i - 1) % lat) for i in range(lat)]
+    send = synthesis_kernel(bands, rows, lane_rows, steps, lat, lon)(
+        *place, wavenumbers, love_factor, got, pltpu.with_memory_space_constraint(values, pltpu.HBM))
+    send, bottom, top, side = lax.optimization_barrier((send, bottom, top, side))
+    up = [(i, i + 1) for i in range(lat - 1)]
+    down = [(i + 1, i) for i in range(lat - 1)]
+    got = lax.all_to_all(send, ("lat", "lon"), split_axis=0, concat_axis=0, tiled=True)
     low = lax.ppermute(bottom, "lat", up)
     high = lax.ppermute(top, "lat", down)
     low_side = lax.ppermute(side, "lon", [(i, (i + 1) % lon) for i in range(lon)])
     high_side = low_side if lon == 2 else lax.ppermute(
         side, "lon", [(i, (i - 1) % lon) for i in range(lon)])
-    send = synthesis_kernel(bands, rows, lane_rows, steps, lat, lon)(
-        *place, wavenumbers, love_factor, got, pltpu.with_memory_space_constraint(values, pltpu.HBM))
-    got = lax.all_to_all(send, ("lat", "lon"), split_axis=0, concat_axis=0, tiled=True)
     got = got.reshape(lat, lon, 2, lane_rows)[:, :2]
     return step_kernel(rows, cols, width, lat, waves, lane_rows)(
         *place, got, table, low, high, low_side, high_side,

time: 56.9 us -> 60.5 us (1.063)
  waiting for transfers between devices: 7.22 us -> 8.95 us
  starting transfers between devices: 15.8 us -> 17.5 us
    all_to_all x2, starting transfers between devices: 9.92 us -> 13.5 us  [local(): lax.all_to_all(send, ('lat', 'lon'), split_axis=0, concat_axis=0, tiled=T...]
    ppermute x1, starting transfers between devices: 3.85 us -> 1.29 us  [local(): high = lax.ppermute(top, 'lat', down)]
    all_to_all x2, waiting for transfers between devices: 6.03 us -> 7.89 us  [local(): lax.all_to_all(send, ('lat', 'lon'), split_axis=0, concat_axis=0, tiled=T...]
  transfers between devices with their start and end apart: 5 -> 5, of which waited for: 2 -> 3; matrix products, arithmetic and copies ran while one was open for 0% -> 0% of each run, Pallas kernels for 20% -> 9%
where the time goes in v1:
time: 60.5 us; the launch traced here: 60.2 us
  Pallas kernels  32.9 us (54%)
  starting transfers between devices  17.5 us (29%)
  waiting for transfers between devices  8.95 us (15%)
  between operations  0.78 us (1%)
    pallas_call x1, Pallas kernels, local(): step_kernel(rows, cols, width, lat, waves, lane_rows)  15.1 us
    all_to_all x2, starting transfers between devices, local(): lax.all_to_all(send, ('lat', 'lon'), split_axis=0, concat_axis=0, tiled=T...  13.5 us
    all_to_all x2, waiting for transfers between devices, local(): lax.all_to_all(send, ('lat', 'lon'), split_axis=0, concat_axis=0, tiled=T...  7.89 us
    pallas_call x1, Pallas kernels, local(): edge_kernel(rows, cols, width, lat, lon, waves, lane_rows)  6.61 us
    pallas_call x1, Pallas kernels, local(): synthesis_kernel(bands, rows, lane_rows, steps, lat, lon)  5.75 us
    pallas_call x1, Pallas kernels, local(): values = legendre_kernel(bands, rows, lane_rows, steps)(*place, wavenumbers)  5.49 us
    ppermute x1, starting transfers between devices, local(): low = lax.ppermute(bottom, 'lat', up)  2.34 us
    ppermute x1, starting transfers between devices, local(): high = lax.ppermute(top, 'lat', down)  1.29 us
  transfers between devices with their start and end apart: 5, of which 3 were waited for; matrix products, arithmetic and copies ran while one was open for 0% of the time, Pallas kernels for 9%

profile of v1, /device:TPU:0, one launch (start us, length us, event | category | flops | bytes accessed | tf_op | source)
XLA Modules:
  0.0 60.2 jit_solution(4981625851041690867)
XLA Ops:
  0.6 0.0 copy-start.2
  0.6 6.6 %edge_fourier.1 = (f32[32,2,256]{2,1,0:T(2,128)}, f32[8,4320]{1,0:T(8,128)}, f32[8,4320]{1,0:T(8,128)}, f32[192,128]{1,0:T(8,128)}, bf16[96,4480]{1,0:T(8,128)(2,1)}) custom-call(s32[1]{0:T(128)} %bitcast.band_ref, s32[1]{0:T(128)} %bitcast.1.sector_ref, s32[16]{0:T(128)} %waves_ref.5, f32[1,192,4320]{2,1,0:T(8,128)} %elev.3, f32[1,2,192,4320]{3,2,1,0:T(8,128)} %vel.3, ...), custom_call_target="tpu_custom_call" | custom-call | tf_op jit(solution)/shard_map/edge_fourier/pallas_call | solution.py:647
  7.3 0.0 copy-start.1
  7.3 7.3 %all-to-all-start = ((f32[32,2,256]{2,1,0:T(2,128)}), f32[32,2,256]{2,1,0:T(2,128)S(1)}, u32[]{:S(2)}, u32[]{:S(2)}) async-start(f32[32,2,256]{2,1,0:T(2,128)} %get-tuple-element.12), calls=%async_computation | async-start | bytes 131072 | tf_op jit(solution)/shard_map/all_to_all | solution.py:649
  14.6 0.0 copy-done.2
  14.6 5.5 %legendre_values.1.values_in = f32[544,8,256]{2,1,0:T(8,128)} custom-call(s32[1]{0:T(128)} %bitcast.band_ref, s32[1]{0:T(128)} %bitcast.1.sector_ref, s32[16]{0:T(128)S(1)} %copy-done.2), custom_call_target="tpu_custom_call" | custom-call | flops 13369344 | bytes 4456448 | tf_op jit(solution)/shard_map/legendre_values/pallas_call | solution.py:650
  20.1 0.0 copy-start.4
  20.1 0.0 copy-start.3
  20.1 0.0 copy-start.5
  20.1 0.0 copy-start
  20.2 1.9 %all-to-all-done.got = f32[32,2,256]{2,1,0:T(2,128)S(1)} async-done(((f32[32,2,256]{2,1,0:T(2,128)}), f32[32,2,256]{2,1,0:T(2,128)S(1)}, u32[]{:S(2)}, u32[]{:S(2)}) %all-to-all-start) | async-done | bytes 65568 | tf_op jit(solution)/shard_map/all_to_all | solution.py:649
  22.0 0.0 copy-done.1
  22.0 5.7 %degree_sums.1 = f32[32,2,256]{2,1,0:T(2,128)} custom-call(s32[1]{0:T(128)} %bitcast.band_ref, s32[1]{0:T(128)} %bitcast.1.sector_ref, s32[16]{0:T(128)S(1)} %copy-done.2, f32[1081]{0:T(1024)S(1)} %copy-done.1, f32[32,2,256]{2,1,0:T(2,128)S(1)} %all-to-all-done.got, f32[544,8,256]{2,1,0:T(8,128)} %legendre_values.1.values_in), custom_call_target="tpu_custom_call" | custom-call | tf_op jit(solution)/shard_map/degree_sums/pallas_call | solution.py:651
  27.8 0.0 copy-done.4
  27.8 2.3 %collective-permute-start = (f32[8,4320]{1,0:T(8,128)S(1)}, f32[8,4320]{1,0:T(8,128)S(1)}, u32[]{:S(2)}, u32[]{:S(2)}) collective-permute-start(f32[8,4320]{1,0:T(8,128)S(1)} %copy-done.4), channel_id=1, source_target_pairs={{0,2},{2,4},{4,6},{6,8},{8,10},{10,12},{12,14},{14,16},{16,18},{18... | collective-permute-start | bytes 414728 | tf_op jit(solution)/shard_map/ppermute | solution.py:657
  30.1 0.0 copy-done.3
  30.2 1.3 %collective-permute-start.1 = (f32[8,4320]{1,0:T(8,128)S(1)}, f32[8,4320]{1,0:T(8,128)S(1)}, u32[]{:S(2)}, u32[]{:S(2)}) collective-permute-start(f32[8,4320]{1,0:T(8,128)S(1)} %copy-done.3), channel_id=1, source_target_pairs={{2,0},{4,2},{6,4},{8,6},{10,8},{12,10},{14,12},{16,14},{18,16},{20... | collective-permute-start | bytes 414728 | tf_op jit(solution)/shard_map/ppermute | solution.py:658
  31.5 6.2 %all-to-all-start.1 = ((f32[32,2,256]{2,1,0:T(2,128)}), f32[32,2,256]{2,1,0:T(2,128)S(1)}, u32[]{:S(2)}, u32[]{:S(2)}) async-start(f32[32,2,256]{2,1,0:T(2,128)} %degree_sums.1), calls=%async_computation.1 | async-start | bytes 131072 | tf_op jit(solution)/shard_map/all_to_all | solution.py:656
  37.7 0.0 copy-done.5
  37.7 0.3 collective-permute-start.2
  38.0 1.1 %collective-permute-done.2.low_side.high_side = f32[192,128]{1,0:T(8,128)S(1)} collective-permute-done((f32[192,128]{1,0:T(8,128)S(1)}, f32[192,128]{1,0:T(8,128)S(1)}, u32[]{:S(2)}, u32[]{:S(2)}) %collective-permute-start.2) | collective-permute-done | bytes 98336 | tf_op jit(solution)/shard_map/ppermute | solution.py:659
  39.0 6.0 %all-to-all-done.1 = f32[32,2,256]{2,1,0:T(2,128)S(1)} async-done(((f32[32,2,256]{2,1,0:T(2,128)}), f32[32,2,256]{2,1,0:T(2,128)S(1)}, u32[]{:S(2)}, u32[]{:S(2)}) %all-to-all-start.1) | async-done | bytes 65568 | tf_op jit(solution)/shard_map/all_to_all | solution.py:656
  45.1 0.0 collective-permute-done.low
  45.1 0.0 collective-permute-done.1.high
  45.1 0.0 copy-done
  45.1 15.1 %surge_step.1 = (f32[1,192,4320]{2,1,0:T(8,128)}, f32[1,2,192,4320]{3,2,1,0:T(8,128)}, f32[1,192,4320]{2,1,0:T(8,128)}) custom-call(s32[1]{0:T(128)} %bitcast.band_ref, s32[1]{0:T(128)} %bitcast.1.sector_ref, f32[16,2,2,256]{3,2,1,0:T(2,128)S(1)} %bitcast.3, bf16[96,4480]{1,0:T(8,128)(2,1)S(1)} %copy-done, f32[8,4320]{1,0:T(8,128)S(1)} %collective-permute-done.low, ...), custom_call_target="tpu_custom_call" | custom-call | tf_op jit(solution)/shard_map/surge_step/pallas_call | solution.py:663
Async XLA Ops:
  0.6 14.0 %copy-start.2 = (s32[16]{0:T(128)S(1)}, s32[16]{0:T(128)}, u32[]{:S(2)}) copy-start(s32[16]{0:T(128)} %waves_ref.5) | copy-start | bytes 196
  7.3 14.8 %copy-start.1 = (f32[1081]{0:T(1024)S(1)}, f32[1081]{0:T(1024)}, u32[]{:S(2)}) copy-start(f32[1081]{0:T(1024)} %love.1) | copy-start | bytes 12976
  7.3 14.7 %all-to-all-start = ((f32[32,2,256]{2,1,0:T(2,128)}), f32[32,2,256]{2,1,0:T(2,128)S(1)}, u32[]{:S(2)}, u32[]{:S(2)}) async-start(f32[32,2,256]{2,1,0:T(2,128)} %get-tuple-element.12), calls=%async_computation | async-start | bytes 131072 | tf_op jit(solution)/shard_map/all_to_all | solution.py:649
  20.1 7.7 %copy-start.4 = (f32[8,4320]{1,0:T(8,128)S(1)}, f32[8,4320]{1,0:T(8,128)}, u32[]{:S(2)}) copy-start(f32[8,4320]{1,0:T(8,128)} %get-tuple-element.18) | copy-start | bytes 414724
  20.1 10.0 %copy-start.3 = (f32[8,4320]{1,0:T(8,128)S(1)}, f32[8,4320]{1,0:T(8,128)}, u32[]{:S(2)}) copy-start(f32[8,4320]{1,0:T(8,128)} %get-tuple-element.19) | copy-start | bytes 414724
  20.1 17.5 %copy-start.5 = (f32[192,128]{1,0:T(8,128)S(1)}, f32[192,128]{1,0:T(8,128)}, u32[]{:S(2)}) copy-start(f32[192,128]{1,0:T(8,128)} %get-tuple-element.20) | copy-start | bytes 294916
  20.1 24.9 %copy-start = (bf16[96,4480]{1,0:T(8,128)(2,1)S(1)}, bf16[96,4480]{1,0:T(8,128)(2,1)}, u32[]{:S(2)}) copy-start(bf16[96,4480]{1,0:T(8,128)(2,1)} %get-tuple-element.17.table) | copy-start | bytes 2580484
  27.8 17.3 %collective-permute-start = (f32[8,4320]{1,0:T(8,128)S(1)}, f32[8,4320]{1,0:T(8,128)S(1)}, u32[]{:S(2)}, u32[]{:S(2)}) collective-permute-start(f32[8,4320]{1,0:T(8,128)S(1)} %copy-done.4), channel_id=1, source_target_pairs={{0,2},{2,4},{4,6},{6,8},{8,10},{10,12},{12,14},{14,16},{16,18},{18... | collective-permute-start | bytes 414728 | tf_op jit(solution)/shard_map/ppermute | solution.py:657
  30.2 14.9 %collective-permute-start.1 = (f32[8,4320]{1,0:T(8,128)S(1)}, f32[8,4320]{1,0:T(8,128)S(1)}, u32[]{:S(2)}, u32[]{:S(2)}) collective-permute-start(f32[8,4320]{1,0:T(8,128)S(1)} %copy-done.3), channel_id=1, source_target_pairs={{2,0},{4,2},{6,4},{8,6},{10,8},{12,10},{14,12},{16,14},{18,16},{20... | collective-permute-start | bytes 414728 | tf_op jit(solution)/shard_map/ppermute | solution.py:658
  31.5 13.6 %all-to-all-start.1 = ((f32[32,2,256]{2,1,0:T(2,128)}), f32[32,2,256]{2,1,0:T(2,128)S(1)}, u32[]{:S(2)}, u32[]{:S(2)}) async-start(f32[32,2,256]{2,1,0:T(2,128)} %degree_sums.1), calls=%async_computation.1 | async-start | bytes 131072 | tf_op jit(solution)/shard_map/all_to_all | solution.py:656
  37.7 1.4 %collective-permute-start.2 = (f32[192,128]{1,0:T(8,128)S(1)}, f32[192,128]{1,0:T(8,128)S(1)}, u32[]{:S(2)}, u32[]{:S(2)}) collective-permute-start(f32[192,128]{1,0:T(8,128)S(1)} %copy-done.5), channel_id=1, source_target_pairs={{0,1},{1,0},{2,3},{3,2},{4,5},{5,4},{6,7},{7,6},{8,9},{9,8},{10,11... | collective-permute-start | bytes 294920 | tf_op jit(solution)/shard_map/ppermute | solution.py:659

commit v2 on v0

--- a/solution.py
+++ b/solution.py
@@ -443,8 +443,11 @@
         elev_v[top - 2 : top, :] = low[0:2, :]
         elev_v[top + rows : top + rows + 2, :] = high[0:2, :]
         for n, buffer in enumerate((u_v, v_v, wy_v, depth_v, wet_v)):
-            buffer[top - 1 : top, :] = low[2 + n : 3 + n, :].astype(buffer.dtype)
-            buffer[top + rows : top + rows + 1, :] = high[2 + n : 3 + n, :].astype(buffer.dtype)
+            before, behind = low[2 + n : 3 + n, :], high[2 + n : 3 + n, :]
+            if buffer is depth_v:
+                before, behind = jnp.maximum(before, 0.2), jnp.maximum(behind, 0.2)
+            buffer[top - 1 : top, :] = before.astype(buffer.dtype)
+            buffer[top + rows : top + rows + 1, :] = behind.astype(buffer.dtype)
 
         group = 4
         after = slice(top + rows, top + rows + 2)
@@ -646,10 +649,8 @@
     got = lax.all_to_all(send, ("lat", "lon"), split_axis=0, concat_axis=0, tiled=True)
     values = legendre_kernel(bands, rows, lane_rows, steps)(*place, wavenumbers)
     values, bottom, top, side = lax.optimization_barrier((values, bottom, top, side))
-    up = [(i, (i + 1) % lat) for i in range(lat)]
-    down = [(i, (i - 1) % lat) for i in range(lat)]
-    low = lax.ppermute(bottom, "lat", up)
-    high = lax.ppermute(top, "lat", down)
+    low = lax.ppermute(bottom, "lat", [(i, i + 1) for i in range(lat - 1)])
+    high = lax.ppermute(top, "lat", [(i + 1, i) for i in range(lat - 1)])
     low_side = lax.ppermute(side, "lon", [(i, (i + 1) % lon) for i in range(lon)])
     high_side = low_side if lon == 2 else lax.ppermute(
         side, "lon", [(i, (i - 1) % lon) for i in range(lon)])

time: 56.9 us -> 60.6 us (1.065)
  starting transfers between devices: 15.8 us -> 19.5 us
    all_to_all x2, starting transfers between devices: 9.92 us -> 14 us  [local(): lax.all_to_all(send, ('lat', 'lon'), split_axis=0, concat_axis=0, tiled=T...]
  transfers between devices with their start and end apart: 5 -> 5, of which waited for: 2 -> 2; matrix products, arithmetic and copies ran while one was open for 0% -> 0% of each run, Pallas kernels for 20% -> 19%
where the time goes in v2:
time: 60.6 us; the launch traced here: 60.3 us
  Pallas kernels  32.9 us (54%)
  starting transfers between devices  19.5 us (32%)
  waiting for transfers between devices  7.08 us (12%)
  between operations  0.79 us (1%)
    pallas_call x1, Pallas kernels, local(): step_kernel(rows, cols, width, lat, waves, lane_rows)  15.1 us
    all_to_all x2, starting transfers between devices, local(): lax.all_to_all(send, ('lat', 'lon'), split_axis=0, concat_axis=0, tiled=T...  14 us
    pallas_call x1, Pallas kernels, local(): edge_kernel(rows, cols, width, lat, lon, waves, lane_rows)  6.61 us
    all_to_all x2, waiting for transfers between devices, local(): lax.all_to_all(send, ('lat', 'lon'), split_axis=0, concat_axis=0, tiled=T...  6.03 us
    pallas_call x1, Pallas kernels, local(): synthesis_kernel(bands, rows, lane_rows, steps, lat, lon)  5.76 us
    pallas_call x1, Pallas kernels, local(): values = legendre_kernel(bands, rows, lane_rows, steps)(*place, wavenumbers)  5.49 us
    ppermute x1, starting transfers between devices, local(): low = lax.ppermute(bottom, 'lat', [(i, i + 1) for i in range(lat - 1)])  3.81 us
    ppermute x1, starting transfers between devices, local(): high = lax.ppermute(top, 'lat', [(i + 1, i) for i in range(lat - 1)])  1.29 us
  transfers between devices with their start and end apart: 5, of which 2 were waited for; matrix products, arithmetic and copies ran while one was open for 0% of the time, Pallas kernels for 19%

profile of v2, /device:TPU:0, one launch (start us, length us, event | category | flops | bytes accessed | tf_op | source)
XLA Modules:
  0.0 60.3 jit_solution(10423762104027887710)
XLA Ops:
  0.6 0.0 copy-start.2
  0.6 6.6 %edge_fourier.1 = (f32[32,2,256]{2,1,0:T(2,128)}, f32[8,4320]{1,0:T(8,128)}, f32[8,4320]{1,0:T(8,128)}, f32[192,128]{1,0:T(8,128)}, bf16[96,4480]{1,0:T(8,128)(2,1)}) custom-call(s32[1]{0:T(128)} %bitcast.band_ref, s32[1]{0:T(128)} %bitcast.1.sector_ref, s32[16]{0:T(128)} %waves_ref.5, f32[1,192,4320]{2,1,0:T(8,128)} %elev.3, f32[1,2,192,4320]{3,2,1,0:T(8,128)} %vel.3, ...), custom_call_target="tpu_custom_call" | custom-call | tf_op jit(solution)/shard_map/edge_fourier/pallas_call | solution.py:647
  7.3 0.0 copy-start.4
  7.3 0.0 copy-start.3
  7.3 0.0 copy-start.1
  7.3 7.3 %all-to-all-start = ((f32[32,2,256]{2,1,0:T(2,128)}), f32[32,2,256]{2,1,0:T(2,128)S(1)}, u32[]{:S(2)}, u32[]{:S(2)}) async-start(f32[32,2,256]{2,1,0:T(2,128)} %get-tuple-element.12), calls=%async_computation | async-start | bytes 131072 | tf_op jit(solution)/shard_map/all_to_all | solution.py:649
  14.6 0.0 copy-done.2
  14.6 5.5 %legendre_values.1.values_in = f32[544,8,256]{2,1,0:T(8,128)} custom-call(s32[1]{0:T(128)} %bitcast.band_ref, s32[1]{0:T(128)} %bitcast.1.sector_ref, s32[16]{0:T(128)S(1)} %copy-done.2), custom_call_target="tpu_custom_call" | custom-call | flops 13369344 | bytes 4456448 | tf_op jit(solution)/shard_map/legendre_values/pallas_call | solution.py:650
  20.1 0.0 copy-start.5
  20.1 0.0 copy-start
  20.2 0.0 copy-done.4
  20.2 3.8 %collective-permute-start = (f32[8,4320]{1,0:T(8,128)S(1)}, f32[8,4320]{1,0:T(8,128)S(1)}, u32[]{:S(2)}, u32[]{:S(2)}) collective-permute-start(f32[8,4320]{1,0:T(8,128)S(1)} %copy-done.4), channel_id=1, source_target_pairs={{0,2},{2,4},{4,6},{6,8},{8,10},{10,12},{12,14},{14,16},{16,18},{18... | collective-permute-start | bytes 414728 | tf_op jit(solution)/shard_map/ppermute | solution.py:652
  24.0 0.0 copy-done.3
  24.0 1.3 %collective-permute-start.1 = (f32[8,4320]{1,0:T(8,128)S(1)}, f32[8,4320]{1,0:T(8,128)S(1)}, u32[]{:S(2)}, u32[]{:S(2)}) collective-permute-start(f32[8,4320]{1,0:T(8,128)S(1)} %copy-done.3), channel_id=1, source_target_pairs={{2,0},{4,2},{6,4},{8,6},{10,8},{12,10},{14,12},{16,14},{18,16},{20... | collective-permute-start | bytes 414728 | tf_op jit(solution)/shard_map/ppermute | solution.py:653
  25.3 0.0 all-to-all-done.got
  25.3 0.0 copy-done.1
  25.3 5.8 %degree_sums.1 = f32[32,2,256]{2,1,0:T(2,128)} custom-call(s32[1]{0:T(128)} %bitcast.band_ref, s32[1]{0:T(128)} %bitcast.1.sector_ref, s32[16]{0:T(128)S(1)} %copy-done.2, f32[1081]{0:T(1024)S(1)} %copy-done.1, f32[32,2,256]{2,1,0:T(2,128)S(1)} %all-to-all-done.got, f32[544,8,256]{2,1,0:T(8,128)} %legendre_values.1.values_in), custom_call_target="tpu_custom_call" | custom-call | tf_op jit(solution)/shard_map/degree_sums/pallas_call | solution.py:657
  31.1 6.7 %all-to-all-start.1 = ((f32[32,2,256]{2,1,0:T(2,128)}), f32[32,2,256]{2,1,0:T(2,128)S(1)}, u32[]{:S(2)}, u32[]{:S(2)}) async-start(f32[32,2,256]{2,1,0:T(2,128)} %degree_sums.1), calls=%async_computation.1 | async-start | bytes 131072 | tf_op jit(solution)/shard_map/all_to_all | solution.py:659
  37.8 0.0 copy-done.5
  37.8 0.3 collective-permute-start.2
  38.1 1.1 %collective-permute-done.2.low_side.high_side = f32[192,128]{1,0:T(8,128)S(1)} collective-permute-done((f32[192,128]{1,0:T(8,128)S(1)}, f32[192,128]{1,0:T(8,128)S(1)}, u32[]{:S(2)}, u32[]{:S(2)}) %collective-permute-start.2) | collective-permute-done | bytes 98336 | tf_op jit(solution)/shard_map/ppermute | solution.py:654
  39.2 0.0 collective-permute-done.low
  39.2 0.0 collective-permute-done.1.high
  39.2 6.0 %all-to-all-done.1 = f32[32,2,256]{2,1,0:T(2,128)S(1)} async-done(((f32[32,2,256]{2,1,0:T(2,128)}), f32[32,2,256]{2,1,0:T(2,128)S(1)}, u32[]{:S(2)}, u32[]{:S(2)}) %all-to-all-start.1) | async-done | bytes 65568 | tf_op jit(solution)/shard_map/all_to_all | solution.py:659
  45.2 0.0 copy-done
  45.2 15.1 %surge_step.1 = (f32[1,192,4320]{2,1,0:T(8,128)}, f32[1,2,192,4320]{3,2,1,0:T(8,128)}, f32[1,192,4320]{2,1,0:T(8,128)}) custom-call(s32[1]{0:T(128)} %bitcast.band_ref, s32[1]{0:T(128)} %bitcast.1.sector_ref, f32[16,2,2,256]{3,2,1,0:T(2,128)S(1)} %bitcast.3, bf16[96,4480]{1,0:T(8,128)(2,1)S(1)} %copy-done, f32[8,4320]{1,0:T(8,128)S(1)} %collective-permute-done.low, ...), custom_call_target="tpu_custom_call" | custom-call | tf_op jit(solution)/shard_map/surge_step/pallas_call | solution.py:661
Async XLA Ops:
  0.6 14.0 %copy-start.2 = (s32[16]{0:T(128)S(1)}, s32[16]{0:T(128)}, u32[]{:S(2)}) copy-start(s32[16]{0:T(128)} %waves_ref.5) | copy-start | bytes 196
  7.3 12.9 %copy-start.4 = (f32[8,4320]{1,0:T(8,128)S(1)}, f32[8,4320]{1,0:T(8,128)}, u32[]{:S(2)}) copy-start(f32[8,4320]{1,0:T(8,128)} %get-tuple-element.18) | copy-start | bytes 414724
  7.3 16.7 %copy-start.3 = (f32[8,4320]{1,0:T(8,128)S(1)}, f32[8,4320]{1,0:T(8,128)}, u32[]{:S(2)}) copy-start(f32[8,4320]{1,0:T(8,128)} %get-tuple-element.19) | copy-start | bytes 414724
  7.3 18.0 %copy-start.1 = (f32[1081]{0:T(1024)S(1)}, f32[1081]{0:T(1024)}, u32[]{:S(2)}) copy-start(f32[1081]{0:T(1024)} %love.1) | copy-start | bytes 12976
  7.3 18.0 %all-to-all-start = ((f32[32,2,256]{2,1,0:T(2,128)}), f32[32,2,256]{2,1,0:T(2,128)S(1)}, u32[]{:S(2)}, u32[]{:S(2)}) async-start(f32[32,2,256]{2,1,0:T(2,128)} %get-tuple-element.12), calls=%async_computation | async-start | bytes 131072 | tf_op jit(solution)/shard_map/all_to_all | solution.py:649
  20.1 17.7 %copy-start.5 = (f32[192,128]{1,0:T(8,128)S(1)}, f32[192,128]{1,0:T(8,128)}, u32[]{:S(2)}) copy-start(f32[192,128]{1,0:T(8,128)} %get-tuple-element.20) | copy-start | bytes 294916
  20.1 25.1 %copy-start = (bf16[96,4480]{1,0:T(8,128)(2,1)S(1)}, bf16[96,4480]{1,0:T(8,128)(2,1)}, u32[]{:S(2)}) copy-start(bf16[96,4480]{1,0:T(8,128)(2,1)} %get-tuple-element.17.table) | copy-start | bytes 2580484
  20.2 19.0 %collective-permute-start = (f32[8,4320]{1,0:T(8,128)S(1)}, f32[8,4320]{1,0:T(8,128)S(1)}, u32[]{:S(2)}, u32[]{:S(2)}) collective-permute-start(f32[8,4320]{1,0:T(8,128)S(1)} %copy-done.4), channel_id=1, source_target_pairs={{0,2},{2,4},{4,6},{6,8},{8,10},{10,12},{12,14},{14,16},{16,18},{18... | collective-permute-start | bytes 414728 | tf_op jit(solution)/shard_map/ppermute | solution.py:652
  24.0 15.2 %collective-permute-start.1 = (f32[8,4320]{1,0:T(8,128)S(1)}, f32[8,4320]{1,0:T(8,128)S(1)}, u32[]{:S(2)}, u32[]{:S(2)}) collective-permute-start(f32[8,4320]{1,0:T(8,128)S(1)} %copy-done.3), channel_id=1, source_target_pairs={{2,0},{4,2},{6,4},{8,6},{10,8},{12,10},{14,12},{16,14},{18,16},{20... | collective-permute-start | bytes 414728 | tf_op jit(solution)/shard_map/ppermute | solution.py:653
  31.1 14.1 %all-to-all-start.1 = ((f32[32,2,256]{2,1,0:T(2,128)}), f32[32,2,256]{2,1,0:T(2,128)S(1)}, u32[]{:S(2)}, u32[]{:S(2)}) async-start(f32[32,2,256]{2,1,0:T(2,128)} %degree_sums.1), calls=%async_computation.1 | async-start | bytes 131072 | tf_op jit(solution)/shard_map/all_to_all | solution.py:659
  37.8 1.4 %collective-permute-start.2 = (f32[192,128]{1,0:T(8,128)S(1)}, f32[192,128]{1,0:T(8,128)S(1)}, u32[]{:S(2)}, u32[]{:S(2)}) collective-permute-start(f32[192,128]{1,0:T(8,128)S(1)} %copy-done.5), channel_id=1, source_target_pairs={{0,1},{1,0},{2,3},{3,2},{4,5},{5,4},{6,7},{7,6},{8,9},{9,8},{10,11... | collective-permute-start | bytes 294920 | tf_op jit(solution)/shard_map/ppermute | solution.py:654

commit v3 on v0

--- a/solution.py
+++ b/solution.py
@@ -58,7 +58,7 @@
     tail = cols % LANES or LANES
 
     def body(band_ref, sector_ref, waves_ref, elev, vel, wind, depth, wet,
-             send, top, bottom, side, table, elev_v, wet_v, load_hi, load_lo,
+             send, near, far, side, table, elev_v, wet_v, load_hi, load_lo,
              top_v, bottom_v, left_v, right_v, sems):
         band = band_ref[0]
         sector = sector_ref[0]
@@ -124,15 +124,25 @@
 
         for copy in copies:
             copy.wait()
-        top[0:2, :] = elev_v[0:2, :]
-        bottom[0:2, :] = elev_v[rows - 2 : rows, :]
-        for n in range(4):
-            top[2 + n : 3 + n, :] = top_v[n]
-            bottom[2 + n : 3 + n, :] = bottom_v[n]
-        top[6:7, :] = wet_v[0:1, :].astype(f32)
-        bottom[6:7, :] = wet_v[rows - 1 : rows, :].astype(f32)
-        top[7:8, :] = jnp.zeros((1, cols), f32)
-        bottom[7:8, :] = jnp.zeros((1, cols), f32)
+        odd = band % 2 == 1
+
+        def pack(which, edge, start, line):
+            which[0:2, :] = elev_v[start : start + 2, :]
+            for n in range(4):
+                which[2 + n : 3 + n, :] = edge[n]
+            which[6:7, :] = wet_v[line : line + 1, :].astype(f32)
+            which[7:8, :] = jnp.zeros((1, cols), f32)
+
+        @pl.when(odd)
+        def _():
+            pack(near, top_v, 0, 0)
+            pack(far, bottom_v, rows - 2, rows - 1)
+
+        @pl.when(jnp.logical_not(odd))
+        def _():
+            pack(near, bottom_v, rows - 2, rows - 1)
+            pack(far, top_v, 0, 0)
+
         blank = jnp.zeros((8, LANES - tail), f32)
         for start in range(0, rows, 8):
             here = slice(start, start + 8)
@@ -398,7 +408,7 @@
     piece = rows // pieces
     names = 6
 
-    def body(band_ref, sector_ref, got, table, low, high, low_side, high_side,
+    def body(band_ref, sector_ref, got, table, near, far, low_side, high_side,
              elev, vel, wind, depth, wet, elev_out, vel_out, load_out,
              elev_v, u_v, v_v, wx_v, wy_v, depth_v, wet_v, surf, flux, load_v,
              left_v, right_v, zonal, sine_v, merid, sems, out_sems):
@@ -440,6 +450,9 @@
             left_v[n, here, :] = pltpu.roll(low_side[...], (124 - 4 * n) % LANES, 1)
             right_v[n, here, :] = pltpu.roll(high_side[...], (tail - 4 * n) % LANES, 1)
 
+        odd = band % 2 == 1
+        low = jnp.where(odd, near[...], far[...])
+        high = jnp.where(odd, far[...], near[...])
         elev_v[top - 2 : top, :] = low[0:2, :]
         elev_v[top + rows : top + rows + 2, :] = high[0:2, :]
         for n, buffer in enumerate((u_v, v_v, wy_v, depth_v, wet_v)):
@@ -641,15 +654,15 @@
         lax.axis_index("lon").astype(jnp.int32)[None],
     )
 
-    send, top, bottom, side, table = edge_kernel(rows, cols, width, lat, lon, waves, lane_rows)(
+    send, first, second, side, table = edge_kernel(rows, cols, width, lat, lon, waves, lane_rows)(
         *place, wavenumbers, elevation, velocity, wind_forcing, ocean_depth, wet_mask)
     got = lax.all_to_all(send, ("lat", "lon"), split_axis=0, concat_axis=0, tiled=True)
     values = legendre_kernel(bands, rows, lane_rows, steps)(*place, wavenumbers)
-    values, bottom, top, side = lax.optimization_barrier((values, bottom, top, side))
-    up = [(i, (i + 1) % lat) for i in range(lat)]
-    down = [(i, (i - 1) % lat) for i in range(lat)]
-    low = lax.ppermute(bottom, "lat", up)
-    high = lax.ppermute(top, "lat", down)
+    values, first, second, side = lax.optimization_barrier((values, first, second, side))
+    pairs = [(i, i ^ 1) for i in range(lat)]
+    others = [(i, min(max(i - 1 + 2 * (i % 2), 0), lat - 1)) for i in range(lat)]
+    near = lax.ppermute(first, "lat", pairs)
+    far = lax.ppermute(second, "lat", others)
     low_side = lax.ppermute(side, "lon", [(i, (i + 1) % lon) for i in range(lon)])
     high_side = low_side if lon == 2 else lax.ppermute(
         side, "lon", [(i, (i - 1) % lon) for i in range(lon)])
@@ -658,7 +671,7 @@
     got = lax.all_to_all(send, ("lat", "lon"), split_axis=0, concat_axis=0, tiled=True)
     got = got.reshape(lat, lon, 2, lane_rows)[:, :2]
     return step_kernel(rows, cols, width, lat, waves, lane_rows)(
-        *place, got, table, low, high, low_side, high_side,
+        *place, got, table, near, far, low_side, high_side,
         elevation, velocity, wind_forcing, ocean_depth, wet_mask)
 
 

time: 56.9 us -> 58.6 us (1.030)
  starting transfers between devices: 15.8 us -> 17.5 us
    all_to_all x2, starting transfers between devices: 9.92 us -> 14.7 us  [local(): lax.all_to_all(send, ('lat', 'lon'), split_axis=0, concat_axis=0, tiled=T...]
    ppermute x2, starting transfers between devices: 5.67 us -> 2.49 us  [the longest x1 1.83 us: local(): near = lax.ppermute(first, 'lat', pairs)]
  transfers between devices with their start and end apart: 5 -> 5, of which waited for: 2 -> 2; matrix products, arithmetic and copies ran while one was open for 0% -> 0% of each run, Pallas kernels for 20% -> 19%
where the time goes in v3:
time: 58.6 us; the launch traced here: 58.4 us
  Pallas kernels  33 us (56%)
  starting transfers between devices  17.5 us (30%)
  waiting for transfers between devices  7.08 us (12%)
  between operations  0.77 us (1%)
    pallas_call x1, Pallas kernels, local(): step_kernel(rows, cols, width, lat, waves, lane_rows)  15.1 us
    all_to_all x2, starting transfers between devices, local(): lax.all_to_all(send, ('lat', 'lon'), split_axis=0, concat_axis=0, tiled=T...  14.7 us
    pallas_call x1, Pallas kernels, local(): edge_kernel(rows, cols, width, lat, lon, waves, lane_rows)  6.65 us
    all_to_all x2, waiting for transfers between devices, local(): lax.all_to_all(send, ('lat', 'lon'), split_axis=0, concat_axis=0, tiled=T...  6.03 us
    pallas_call x1, Pallas kernels, local(): synthesis_kernel(bands, rows, lane_rows, steps, lat, lon)  5.76 us
    pallas_call x1, Pallas kernels, local(): values = legendre_kernel(bands, rows, lane_rows, steps)(*place, wavenumbers)  5.49 us
    ppermute x1, starting transfers between devices, local(): near = lax.ppermute(first, 'lat', pairs)  1.83 us
  transfers between devices with their start and end apart: 5, of which 2 were waited for; matrix products, arithmetic and copies ran while one was open for 0% of the time, Pallas kernels for 19%

profile of v3, /device:TPU:0, one launch (start us, length us, event | category | flops | bytes accessed | tf_op | source)
XLA Modules:
  0.0 58.4 jit_solution(8086899617371846797)
XLA Ops:
  0.6 0.0 copy-start.2
  0.6 6.6 %edge_fourier.1 = (f32[32,2,256]{2,1,0:T(2,128)}, f32[8,4320]{1,0:T(8,128)}, f32[8,4320]{1,0:T(8,128)}, f32[192,128]{1,0:T(8,128)}, bf16[96,4480]{1,0:T(8,128)(2,1)}) custom-call(s32[1]{0:T(128)} %bitcast.band_ref, s32[1]{0:T(128)} %bitcast.1.sector_ref, s32[16]{0:T(128)} %waves_ref.5, f32[1,192,4320]{2,1,0:T(8,128)} %elev.3, f32[1,2,192,4320]{3,2,1,0:T(8,128)} %vel.3, ...), custom_call_target="tpu_custom_call" | custom-call | tf_op jit(solution)/shard_map/edge_fourier/pallas_call | solution.py:657
  7.3 0.0 copy-start.4
  7.3 0.0 copy-start.3
  7.3 0.0 copy-start.1
  7.3 7.3 %all-to-all-start = ((f32[32,2,256]{2,1,0:T(2,128)}), f32[32,2,256]{2,1,0:T(2,128)S(1)}, u32[]{:S(2)}, u32[]{:S(2)}) async-start(f32[32,2,256]{2,1,0:T(2,128)} %get-tuple-element.12), calls=%async_computation | async-start | bytes 131072 | tf_op jit(solution)/shard_map/all_to_all | solution.py:659
  14.7 0.0 copy-done.2
  14.7 5.5 %legendre_values.1.values_in = f32[544,8,256]{2,1,0:T(8,128)} custom-call(s32[1]{0:T(128)} %bitcast.band_ref, s32[1]{0:T(128)} %bitcast.1.sector_ref, s32[16]{0:T(128)S(1)} %copy-done.2), custom_call_target="tpu_custom_call" | custom-call | flops 13369344 | bytes 4456448 | tf_op jit(solution)/shard_map/legendre_values/pallas_call | solution.py:660
  20.2 0.0 copy-start.5
  20.2 0.0 copy-start
  20.2 0.0 copy-done.4
  20.2 1.8 %collective-permute-start = (f32[8,4320]{1,0:T(8,128)S(1)}, f32[8,4320]{1,0:T(8,128)S(1)}, u32[]{:S(2)}, u32[]{:S(2)}) collective-permute-start(f32[8,4320]{1,0:T(8,128)S(1)} %copy-done.4), channel_id=1, source_target_pairs={{0,2},{2,0},{4,6},{6,4},{8,10},{10,8},{12,14},{14,12},{16,18},{18,... | collective-permute-start | bytes 414728 | tf_op jit(solution)/shard_map/ppermute | solution.py:664
  22.0 0.0 copy-done.3
  22.0 0.7 %collective-permute-start.1 = (f32[8,4320]{1,0:T(8,128)S(1)}, f32[8,4320]{1,0:T(8,128)S(1)}, u32[]{:S(2)}, u32[]{:S(2)}) collective-permute-start(f32[8,4320]{1,0:T(8,128)S(1)} %copy-done.3), channel_id=1, source_target_pairs={{0,0},{2,4},{4,2},{6,8},{8,6},{10,12},{12,10},{14,16},{16,14},{18,... | collective-permute-start | bytes 414728 | tf_op jit(solution)/shard_map/ppermute | solution.py:665
  22.7 0.0 all-to-all-done.got
  22.7 0.0 copy-done.1
  22.7 5.8 %degree_sums.1 = f32[32,2,256]{2,1,0:T(2,128)} custom-call(s32[1]{0:T(128)} %bitcast.band_ref, s32[1]{0:T(128)} %bitcast.1.sector_ref, s32[16]{0:T(128)S(1)} %copy-done.2, f32[1081]{0:T(1024)S(1)} %copy-done.1, f32[32,2,256]{2,1,0:T(2,128)S(1)} %all-to-all-done.got, f32[544,8,256]{2,1,0:T(8,128)} %legendre_values.1.values_in), custom_call_target="tpu_custom_call" | custom-call | tf_op jit(solution)/shard_map/degree_sums/pallas_call | solution.py:669
  28.5 7.3 %all-to-all-start.1 = ((f32[32,2,256]{2,1,0:T(2,128)}), f32[32,2,256]{2,1,0:T(2,128)S(1)}, u32[]{:S(2)}, u32[]{:S(2)}) async-start(f32[32,2,256]{2,1,0:T(2,128)} %degree_sums.1), calls=%async_computation.1 | async-start | bytes 131072 | tf_op jit(solution)/shard_map/all_to_all | solution.py:671
  35.8 0.0 copy-done.5
  35.9 0.3 collective-permute-start.2
  36.2 1.1 %collective-permute-done.2.low_side.high_side = f32[192,128]{1,0:T(8,128)S(1)} collective-permute-done((f32[192,128]{1,0:T(8,128)S(1)}, f32[192,128]{1,0:T(8,128)S(1)}, u32[]{:S(2)}, u32[]{:S(2)}) %collective-permute-start.2) | collective-permute-done | bytes 98336 | tf_op jit(solution)/shard_map/ppermute | solution.py:666
  37.2 0.0 collective-permute-done.near
  37.2 0.0 collective-permute-done.1.far
  37.2 6.0 %all-to-all-done.1 = f32[32,2,256]{2,1,0:T(2,128)S(1)} async-done(((f32[32,2,256]{2,1,0:T(2,128)}), f32[32,2,256]{2,1,0:T(2,128)S(1)}, u32[]{:S(2)}, u32[]{:S(2)}) %all-to-all-start.1) | async-done | bytes 65568 | tf_op jit(solution)/shard_map/all_to_all | solution.py:671
  43.3 0.0 copy-done
  43.3 15.1 %surge_step.1 = (f32[1,192,4320]{2,1,0:T(8,128)}, f32[1,2,192,4320]{3,2,1,0:T(8,128)}, f32[1,192,4320]{2,1,0:T(8,128)}) custom-call(s32[1]{0:T(128)} %bitcast.band_ref, s32[1]{0:T(128)} %bitcast.1.sector_ref, f32[16,2,2,256]{3,2,1,0:T(2,128)S(1)} %bitcast.3, bf16[96,4480]{1,0:T(8,128)(2,1)S(1)} %copy-done, f32[8,4320]{1,0:T(8,128)S(1)} %collective-permute-done.near, ...), custom_call_target="tpu_custom_call" | custom-call | tf_op jit(solution)/shard_map/surge_step/pallas_call | solution.py:673
Async XLA Ops:
  0.6 14.0 %copy-start.2 = (s32[16]{0:T(128)S(1)}, s32[16]{0:T(128)}, u32[]{:S(2)}) copy-start(s32[16]{0:T(128)} %waves_ref.5) | copy-start | bytes 196
  7.3 12.9 %copy-start.4 = (f32[8,4320]{1,0:T(8,128)S(1)}, f32[8,4320]{1,0:T(8,128)}, u32[]{:S(2)}) copy-start(f32[8,4320]{1,0:T(8,128)} %get-tuple-element.18) | copy-start | bytes 414724
  7.3 14.7 %copy-start.3 = (f32[8,4320]{1,0:T(8,128)S(1)}, f32[8,4320]{1,0:T(8,128)}, u32[]{:S(2)}) copy-start(f32[8,4320]{1,0:T(8,128)} %get-tuple-element.19) | copy-start | bytes 414724
  7.3 15.4 %copy-start.1 = (f32[1081]{0:T(1024)S(1)}, f32[1081]{0:T(1024)}, u32[]{:S(2)}) copy-start(f32[1081]{0:T(1024)} %love.1) | copy-start | bytes 12976
  7.3 15.4 %all-to-all-start = ((f32[32,2,256]{2,1,0:T(2,128)}), f32[32,2,256]{2,1,0:T(2,128)S(1)}, u32[]{:S(2)}, u32[]{:S(2)}) async-start(f32[32,2,256]{2,1,0:T(2,128)} %get-tuple-element.12), calls=%async_computation | async-start | bytes 131072 | tf_op jit(solution)/shard_map/all_to_all | solution.py:659
  20.2 15.7 %copy-start.5 = (f32[192,128]{1,0:T(8,128)S(1)}, f32[192,128]{1,0:T(8,128)}, u32[]{:S(2)}) copy-start(f32[192,128]{1,0:T(8,128)} %get-tuple-element.20) | copy-start | bytes 294916
  20.2 23.1 %copy-start = (bf16[96,4480]{1,0:T(8,128)(2,1)S(1)}, bf16[96,4480]{1,0:T(8,128)(2,1)}, u32[]{:S(2)}) copy-start(bf16[96,4480]{1,0:T(8,128)(2,1)} %get-tuple-element.17.table) | copy-start | bytes 2580484
  20.2 17.0 %collective-permute-start = (f32[8,4320]{1,0:T(8,128)S(1)}, f32[8,4320]{1,0:T(8,128)S(1)}, u32[]{:S(2)}, u32[]{:S(2)}) collective-permute-start(f32[8,4320]{1,0:T(8,128)S(1)} %copy-done.4), channel_id=1, source_target_pairs={{0,2},{2,0},{4,6},{6,4},{8,10},{10,8},{12,14},{14,12},{16,18},{18,... | collective-permute-start | bytes 414728 | tf_op jit(solution)/shard_map/ppermute | solution.py:664
  22.0 15.2 %collective-permute-start.1 = (f32[8,4320]{1,0:T(8,128)S(1)}, f32[8,4320]{1,0:T(8,128)S(1)}, u32[]{:S(2)}, u32[]{:S(2)}) collective-permute-start(f32[8,4320]{1,0:T(8,128)S(1)} %copy-done.3), channel_id=1, source_target_pairs={{0,0},{2,4},{4,2},{6,8},{8,6},{10,12},{12,10},{14,16},{16,14},{18,... | collective-permute-start | bytes 414728 | tf_op jit(solution)/shard_map/ppermute | solution.py:665
  28.5 14.8 %all-to-all-start.1 = ((f32[32,2,256]{2,1,0:T(2,128)}), f32[32,2,256]{2,1,0:T(2,128)S(1)}, u32[]{:S(2)}, u32[]{:S(2)}) async-start(f32[32,2,256]{2,1,0:T(2,128)} %degree_sums.1), calls=%async_computation.1 | async-start | bytes 131072 | tf_op jit(solution)/shard_map/all_to_all | solution.py:671
  35.9 1.4 %collective-permute-start.2 = (f32[192,128]{1,0:T(8,128)S(1)}, f32[192,128]{1,0:T(8,128)S(1)}, u32[]{:S(2)}, u32[]{:S(2)}) collective-permute-start(f32[192,128]{1,0:T(8,128)S(1)} %copy-done.5), channel_id=1, source_target_pairs={{0,1},{1,0},{2,3},{3,2},{4,5},{5,4},{6,7},{7,6},{8,9},{9,8},{10,11... | collective-permute-start | bytes 294920 | tf_op jit(solution)/shard_map/ppermute | solution.py:666

commit v4 on v0

--- a/solution.py
+++ b/solution.py
@@ -56,16 +56,23 @@
 
 def edge_kernel(rows, cols, width, lat, lon, waves, lane_rows):
     tail = cols % LANES or LANES
+    pieces = 4 if rows % 32 == 0 else 1
+    piece = rows // pieces
 
     def body(band_ref, sector_ref, waves_ref, elev, vel, wind, depth, wet,
-             send, top, bottom, side, table, elev_v, wet_v, load_hi, load_lo,
+             send, top, bottom, side, table_out, table, elev_v, wet_v, load_hi, load_lo,
              top_v, bottom_v, left_v, right_v, sems):
         band = band_ref[0]
         sector = sector_ref[0]
-        first = pltpu.make_async_copy(elev.at[0], elev_v, sems.at[0])
-        second = pltpu.make_async_copy(wet, wet_v, sems.at[1])
-        first.start()
-        second.start()
+        main = []
+        for k in range(pieces):
+            here = pl.ds(k * piece, piece)
+            main.append((
+                pltpu.make_async_copy(elev.at[0, here, :], elev_v.at[here, :], sems.at[18 + k]),
+                pltpu.make_async_copy(wet.at[here, :], wet_v.at[here, :], sems.at[18 + pieces + k]),
+            ))
+            for copy in main[k]:
+                copy.start()
         fields = (vel.at[0, 0], vel.at[0, 1], wind.at[1], depth)
         copies = []
         for n, field in enumerate(fields):
@@ -94,9 +101,12 @@
             table[2 * waves : 4 * waves, span] = high
             table[4 * waves : 6 * waves, span] = low
 
-        first.wait()
-        second.wait()
+        table_copy = pltpu.make_async_copy(table, table_out, sems.at[0])
+        table_copy.start()
         for start in range(0, rows, 8):
+            if start % piece == 0:
+                for copy in main[start // piece]:
+                    copy.wait()
             here = slice(start, start + 8)
             high, low = split(elev_v[here, :] * wet_v[here, :].astype(f32))
             load_hi[here, :] = high
@@ -149,6 +159,7 @@
                 moved = pltpu.roll(right[n], (4 * n + 2 - (tail - 2)) % LANES, 1)
                 packed = jnp.where(lane8 // 2 == 2 * n + 1, moved, packed)
             side[here, :] = packed
+        table_copy.wait()
 
     return pl.pallas_call(
         body,
@@ -160,8 +171,9 @@
             jax.ShapeDtypeStruct((6 * waves, width), bf16),
         ),
         in_specs=[SMEM, SMEM, SMEM, ANY, ANY, ANY, ANY, ANY],
-        out_specs=(VMEM, VMEM, VMEM, VMEM, VMEM),
+        out_specs=(VMEM, VMEM, VMEM, VMEM, ANY),
         scratch_shapes=[
+            pltpu.VMEM((6 * waves, width), bf16),
             pltpu.VMEM((rows, cols), f32),
             pltpu.VMEM((rows, cols), jnp.int32),
             pltpu.VMEM((rows, cols), bf16),
@@ -170,7 +182,7 @@
             pltpu.VMEM((4, 1, cols), f32),
             pltpu.VMEM((4, rows, LANES), f32),
             pltpu.VMEM((4, rows, tail), f32),
-            pltpu.SemaphoreType.DMA((18,)),
+            pltpu.SemaphoreType.DMA((18 + 2 * pieces,)),
         ],
         name="edge_fourier",
     )
@@ -289,8 +301,9 @@
 
 
 def synthesis_kernel(bands, rows, lane_rows, steps, lat, lon):
-    parts = 4
+    parts = 2
     share = steps // parts
+    assert share % 16 == 0
 
     def body(band_ref, sector_ref, waves_ref, love, got, values_in, send, mass, totals, values, sems):
         copies = []
@@ -326,23 +339,34 @@
                 out.append(jnp.where(lower, y + pltpu.roll(y, 8 - shift, 0), x + pltpu.roll(x, shift, 0)))
             return out
 
+        held = [[mass[c, r : r + 8, t : t + LANES] for r, t in tiles] for c in range(2)] if len(tiles) <= 4 else None
+
+        def weights(c, i):
+            r, t = tiles[i]
+            return held[c][i] if held else mass[c, r : r + 8, t : t + LANES]
+
         def analyse(n, carry):
-            for c in range(2):
-                parts = []
+            for group in range(2):
+                first = n * 16 + group * 8
+                sums = [[], []]
                 for q in (7, 6, 5, 4, 3, 2, 1, 0):
-                    acc = None
-                    for r, t in tiles:
-                        term = mass[c, r : r + 8, t : t + LANES] * values[n * 8 + q, r : r + 8, t : t + LANES]
-                        acc = term if acc is None else acc + term
-                    parts.append(acc)
-                for shift in (4, 2, 1):
-                    parts = fold(parts, shift)
-                totals[c, pl.ds(n * 8, 8), :] = parts[0]
+                    value = [values[first + q, r : r + 8, t : t + LANES] for r, t in tiles]
+                    for c in range(2):
+                        acc = None
+                        for i, x in enumerate(value):
+                            term = weights(c, i) * x
+                            acc = term if acc is None else acc + term
+                        sums[c].append(acc)
+                for c in range(2):
+                    found = sums[c]
+                    for shift in (4, 2, 1):
+                        found = fold(found, shift)
+                    totals[c, pl.ds(pl.multiple_of(first, 8), 8), :] = found[0]
             return carry
 
         for k in range(parts):
             copies[k].wait()
-            lax.fori_loop(k * share // 8, (k + 1) * share // 8, analyse, 0)
+            lax.fori_loop(k * share // 16, (k + 1) * share // 16, analyse, 0)
         degree = order + parity + 2 * lax.broadcasted_iota(jnp.int32, (steps, LANES), 0)
         weight = jnp.where(degree < DEGREES, 1.0 / (2.0 * degree.astype(f32) + 1.0), 0.0)
         for c in range(2):
@@ -522,7 +546,7 @@
                     d = fetch(t, rows8, 4, depth_v)
                     wet = fetch(t, rows8, 5, wet_v)
                     drag = wet / (d + 0.1 * jnp.sqrt(u * u + v * v))
-                    new_u = drag * (u * d + fetch(t, rows8, 3, wx_v) - (zs * d) * across(*level))
+                    new_u = drag * (fetch(t, rows8, 3, wx_v) + d * (u - zs * across(*level)))
                     keep(wx_v, rows8, t, new_u)
                     flow.append(d * new_u)
                     if t and not (t > cols // LANES and tail == LANES):
@@ -531,7 +555,7 @@
                         else:
                             push = jnp.concatenate(
                                 [wy_v[rows8, cols - tail : cols], jnp.zeros((8, LANES - tail), f32)], axis=1)
-                        new_v = drag * (v * d + push - (meridional * d) * vertical(surf, base, at, level[1]))
+                        new_v = drag * (push + d * (v - meridional * vertical(surf, base, at, level[1])))
                         keep(wy_v, rows8, t, new_v)
                         flux[rows8, at] = sn * d * new_v
                 else:

time: 56.9 us -> 57.2 us (level)
  no operation moved by 1% of the time
where the time goes in v4:
time: 57.2 us; the launch traced here: 56.9 us
  Pallas kernels  33.1 us (58%)
  starting transfers between devices  15.8 us (28%)
  waiting for transfers between devices  7.22 us (13%)
  between operations  0.75 us (1%)
    pallas_call x1, Pallas kernels, local(): step_kernel(rows, cols, width, lat, waves, lane_rows)  15 us
    all_to_all x2, starting transfers between devices, local(): lax.all_to_all(send, ('lat', 'lon'), split_axis=0, concat_axis=0, tiled=T...  9.93 us
    pallas_call x1, Pallas kernels, local(): edge_kernel(rows, cols, width, lat, lon, waves, lane_rows)  6.78 us
    all_to_all x2, waiting for transfers between devices, local(): lax.all_to_all(send, ('lat', 'lon'), split_axis=0, concat_axis=0, tiled=T...  6.03 us
    pallas_call x1, Pallas kernels, local(): synthesis_kernel(bands, rows, lane_rows, steps, lat, lon)  5.91 us
    pallas_call x1, Pallas kernels, local(): values = legendre_kernel(bands, rows, lane_rows, steps)(*place, wavenumbers)  5.49 us
    ppermute x1, starting transfers between devices, local(): high = lax.ppermute(top, 'lat', down)  3.85 us
    ppermute x1, starting transfers between devices, local(): low = lax.ppermute(bottom, 'lat', up)  1.82 us
  transfers between devices with their start and end apart: 5, of which 2 were waited for; matrix products, arithmetic and copies ran while one was open for 0% of the time, Pallas kernels for 20%

profile of v4, /device:TPU:0, one launch (start us, length us, event | category | flops | bytes accessed | tf_op | source)
XLA Modules:
  0.0 56.9 jit_solution(751542581981477583)
XLA Ops:
  0.6 0.0 copy-start.2
  0.6 6.8 %edge_fourier.1 = (f32[32,2,256]{2,1,0:T(2,128)}, f32[8,4320]{1,0:T(8,128)}, f32[8,4320]{1,0:T(8,128)}, f32[192,128]{1,0:T(8,128)}, bf16[96,4480]{1,0:T(8,128)(2,1)}) custom-call(s32[1]{0:T(128)} %bitcast.band_ref, s32[1]{0:T(128)} %bitcast.1.sector_ref, s32[16]{0:T(128)} %waves_ref.5, f32[1,192,4320]{2,1,0:T(8,128)} %elev.3, f32[1,2,192,4320]{3,2,1,0:T(8,128)} %vel.3, ...), custom_call_target="tpu_custom_call" | custom-call | tf_op jit(solution)/shard_map/edge_fourier/pallas_call | solution.py:668
  7.4 0.0 copy-start.4
  7.4 0.0 copy-start.3
  7.5 0.0 copy-start.1
  7.5 7.3 %all-to-all-start = ((f32[32,2,256]{2,1,0:T(2,128)}), f32[32,2,256]{2,1,0:T(2,128)S(1)}, u32[]{:S(2)}, u32[]{:S(2)}) async-start(f32[32,2,256]{2,1,0:T(2,128)} %get-tuple-element.12), calls=%async_computation | async-start | bytes 131072 | tf_op jit(solution)/shard_map/all_to_all | solution.py:670
  14.8 0.0 copy-done.2
  14.8 5.5 %legendre_values.1.values_in = f32[544,8,256]{2,1,0:T(8,128)} custom-call(s32[1]{0:T(128)} %bitcast.band_ref, s32[1]{0:T(128)} %bitcast.1.sector_ref, s32[16]{0:T(128)S(1)} %copy-done.2), custom_call_target="tpu_custom_call" | custom-call | flops 13369344 | bytes 4456448 | tf_op jit(solution)/shard_map/legendre_values/pallas_call | solution.py:671
  20.3 0.0 copy-start.5
  20.3 0.0 copy-start
  20.3 0.0 copy-done.4
  20.3 1.8 %collective-permute-start = (f32[8,4320]{1,0:T(8,128)S(1)}, f32[8,4320]{1,0:T(8,128)S(1)}, u32[]{:S(2)}, u32[]{:S(2)}) collective-permute-start(f32[8,4320]{1,0:T(8,128)S(1)} %copy-done.4), channel_id=1, source_target_pairs={{0,2},{2,4},{4,6},{6,8},{8,10},{10,12},{12,14},{14,16},{16,18},{18... | collective-permute-start | bytes 414728 | tf_op jit(solution)/shard_map/ppermute | solution.py:675
  22.2 0.0 copy-done.3
  22.2 3.9 %collective-permute-start.1 = (f32[8,4320]{1,0:T(8,128)S(1)}, f32[8,4320]{1,0:T(8,128)S(1)}, u32[]{:S(2)}, u32[]{:S(2)}) collective-permute-start(f32[8,4320]{1,0:T(8,128)S(1)} %copy-done.3), channel_id=1, source_target_pairs={{0,30},{2,0},{4,2},{6,4},{8,6},{10,8},{12,10},{14,12},{16,14},{18,... | collective-permute-start | bytes 414728 | tf_op jit(solution)/shard_map/ppermute | solution.py:676
  26.0 0.0 all-to-all-done.got
  26.0 0.0 copy-done.1
  26.0 5.9 %degree_sums.1 = f32[32,2,256]{2,1,0:T(2,128)} custom-call(s32[1]{0:T(128)} %bitcast.band_ref, s32[1]{0:T(128)} %bitcast.1.sector_ref, s32[16]{0:T(128)S(1)} %copy-done.2, f32[1081]{0:T(1024)S(1)} %copy-done.1, f32[32,2,256]{2,1,0:T(2,128)S(1)} %all-to-all-done.got, f32[544,8,256]{2,1,0:T(8,128)} %legendre_values.1.values_in), custom_call_target="tpu_custom_call" | custom-call | tf_op jit(solution)/shard_map/degree_sums/pallas_call | solution.py:680
  32.0 2.6 %all-to-all-start.1 = ((f32[32,2,256]{2,1,0:T(2,128)}), f32[32,2,256]{2,1,0:T(2,128)S(1)}, u32[]{:S(2)}, u32[]{:S(2)}) async-start(f32[32,2,256]{2,1,0:T(2,128)} %degree_sums.1), calls=%async_computation.1 | async-start | bytes 131072 | tf_op jit(solution)/shard_map/all_to_all | solution.py:682
  34.5 0.0 copy-done.5
  34.6 0.2 collective-permute-start.2
  34.7 1.2 %collective-permute-done.2.low_side.high_side = f32[192,128]{1,0:T(8,128)S(1)} collective-permute-done((f32[192,128]{1,0:T(8,128)S(1)}, f32[192,128]{1,0:T(8,128)S(1)}, u32[]{:S(2)}, u32[]{:S(2)}) %collective-permute-start.2) | collective-permute-done | bytes 98336 | tf_op jit(solution)/shard_map/ppermute | solution.py:677
  35.9 0.0 collective-permute-done.low
  35.9 0.0 collective-permute-done.1.high
  35.9 6.0 %all-to-all-done.1 = f32[32,2,256]{2,1,0:T(2,128)S(1)} async-done(((f32[32,2,256]{2,1,0:T(2,128)}), f32[32,2,256]{2,1,0:T(2,128)S(1)}, u32[]{:S(2)}, u32[]{:S(2)}) %all-to-all-start.1) | async-done | bytes 65568 | tf_op jit(solution)/shard_map/all_to_all | solution.py:682
  42.0 0.0 copy-done
  42.0 15.0 %surge_step.1 = (f32[1,192,4320]{2,1,0:T(8,128)}, f32[1,2,192,4320]{3,2,1,0:T(8,128)}, f32[1,192,4320]{2,1,0:T(8,128)}) custom-call(s32[1]{0:T(128)} %bitcast.band_ref, s32[1]{0:T(128)} %bitcast.1.sector_ref, f32[16,2,2,256]{3,2,1,0:T(2,128)S(1)} %bitcast.3, bf16[96,4480]{1,0:T(8,128)(2,1)S(1)} %copy-done, f32[8,4320]{1,0:T(8,128)S(1)} %collective-permute-done.low, ...), custom_call_target="tpu_custom_call" | custom-call | tf_op jit(solution)/shard_map/surge_step/pallas_call | solution.py:684
Async XLA Ops:
  0.6 14.2 %copy-start.2 = (s32[16]{0:T(128)S(1)}, s32[16]{0:T(128)}, u32[]{:S(2)}) copy-start(s32[16]{0:T(128)} %waves_ref.5) | copy-start | bytes 196
  7.4 12.9 %copy-start.4 = (f32[8,4320]{1,0:T(8,128)S(1)}, f32[8,4320]{1,0:T(8,128)}, u32[]{:S(2)}) copy-start(f32[8,4320]{1,0:T(8,128)} %get-tuple-element.18) | copy-start | bytes 414724
  7.4 14.7 %copy-start.3 = (f32[8,4320]{1,0:T(8,128)S(1)}, f32[8,4320]{1,0:T(8,128)}, u32[]{:S(2)}) copy-start(f32[8,4320]{1,0:T(8,128)} %get-tuple-element.19) | copy-start | bytes 414724
  7.5 18.6 %copy-start.1 = (f32[1081]{0:T(1024)S(1)}, f32[1081]{0:T(1024)}, u32[]{:S(2)}) copy-start(f32[1081]{0:T(1024)} %love.1) | copy-start | bytes 12976
  7.5 18.6 %all-to-all-start = ((f32[32,2,256]{2,1,0:T(2,128)}), f32[32,2,256]{2,1,0:T(2,128)S(1)}, u32[]{:S(2)}, u32[]{:S(2)}) async-start(f32[32,2,256]{2,1,0:T(2,128)} %get-tuple-element.12), calls=%async_computation | async-start | bytes 131072 | tf_op jit(solution)/shard_map/all_to_all | solution.py:670
  20.3 14.2 %copy-start.5 = (f32[192,128]{1,0:T(8,128)S(1)}, f32[192,128]{1,0:T(8,128)}, u32[]{:S(2)}) copy-start(f32[192,128]{1,0:T(8,128)} %get-tuple-element.20) | copy-start | bytes 294916
  20.3 21.6 %copy-start = (bf16[96,4480]{1,0:T(8,128)(2,1)S(1)}, bf16[96,4480]{1,0:T(8,128)(2,1)}, u32[]{:S(2)}) copy-start(bf16[96,4480]{1,0:T(8,128)(2,1)} %get-tuple-element.17.table) | copy-start | bytes 2580484
  20.3 15.6 %collective-permute-start = (f32[8,4320]{1,0:T(8,128)S(1)}, f32[8,4320]{1,0:T(8,128)S(1)}, u32[]{:S(2)}, u32[]{:S(2)}) collective-permute-start(f32[8,4320]{1,0:T(8,128)S(1)} %copy-done.4), channel_id=1, source_target_pairs={{0,2},{2,4},{4,6},{6,8},{8,10},{10,12},{12,14},{14,16},{16,18},{18... | collective-permute-start | bytes 414728 | tf_op jit(solution)/shard_map/ppermute | solution.py:675
  22.2 13.8 %collective-permute-start.1 = (f32[8,4320]{1,0:T(8,128)S(1)}, f32[8,4320]{1,0:T(8,128)S(1)}, u32[]{:S(2)}, u32[]{:S(2)}) collective-permute-start(f32[8,4320]{1,0:T(8,128)S(1)} %copy-done.3), channel_id=1, source_target_pairs={{0,30},{2,0},{4,2},{6,4},{8,6},{10,8},{12,10},{14,12},{16,14},{18,... | collective-permute-start | bytes 414728 | tf_op jit(solution)/shard_map/ppermute | solution.py:676
  32.0 10.0 %all-to-all-start.1 = ((f32[32,2,256]{2,1,0:T(2,128)}), f32[32,2,256]{2,1,0:T(2,128)S(1)}, u32[]{:S(2)}, u32[]{:S(2)}) async-start(f32[32,2,256]{2,1,0:T(2,128)} %degree_sums.1), calls=%async_computation.1 | async-start | bytes 131072 | tf_op jit(solution)/shard_map/all_to_all | solution.py:682
  34.6 1.4 %collective-permute-start.2 = (f32[192,128]{1,0:T(8,128)S(1)}, f32[192,128]{1,0:T(8,128)S(1)}, u32[]{:S(2)}, u32[]{:S(2)}) collective-permute-start(f32[192,128]{1,0:T(8,128)S(1)} %copy-done.5), channel_id=1, source_target_pairs={{0,1},{1,0},{2,3},{3,2},{4,5},{5,4},{6,7},{7,6},{8,9},{9,8},{10,11... | collective-permute-start | bytes 294920 | tf_op jit(solution)/shard_map/ppermute | solution.py:677

commit v5 on v1

--- a/solution.py
+++ b/solution.py
@@ -443,11 +443,8 @@
         elev_v[top - 2 : top, :] = low[0:2, :]
         elev_v[top + rows : top + rows + 2, :] = high[0:2, :]
         for n, buffer in enumerate((u_v, v_v, wy_v, depth_v, wet_v)):
-            before, behind = low[2 + n : 3 + n, :], high[2 + n : 3 + n, :]
-            if buffer is depth_v:
-                before, behind = jnp.maximum(before, 0.2), jnp.maximum(behind, 0.2)
-            buffer[top - 1 : top, :] = before.astype(buffer.dtype)
-            buffer[top + rows : top + rows + 1, :] = behind.astype(buffer.dtype)
+            buffer[top - 1 : top, :] = low[2 + n : 3 + n, :].astype(buffer.dtype)
+            buffer[top + rows : top + rows + 1, :] = high[2 + n : 3 + n, :].astype(buffer.dtype)
 
         group = 4
         after = slice(top + rows, top + rows + 2)
@@ -648,14 +645,13 @@
         *place, wavenumbers, elevation, velocity, wind_forcing, ocean_depth, wet_mask)
     got = lax.all_to_all(send, ("lat", "lon"), split_axis=0, concat_axis=0, tiled=True)
     values = legendre_kernel(bands, rows, lane_rows, steps)(*place, wavenumbers)
+    values, bottom = lax.optimization_barrier((values, bottom))
+    low = lax.ppermute(bottom, "lat", [(i, (i + 1) % lat) for i in range(lat)])
     send = synthesis_kernel(bands, rows, lane_rows, steps, lat, lon)(
         *place, wavenumbers, love_factor, got, pltpu.with_memory_space_constraint(values, pltpu.HBM))
-    send, bottom, top, side = lax.optimization_barrier((send, bottom, top, side))
-    up = [(i, i + 1) for i in range(lat - 1)]
-    down = [(i + 1, i) for i in range(lat - 1)]
+    send, top, side = lax.optimization_barrier((send, top, side))
     got = lax.all_to_all(send, ("lat", "lon"), split_axis=0, concat_axis=0, tiled=True)
-    low = lax.ppermute(bottom, "lat", up)
-    high = lax.ppermute(top, "lat", down)
+    high = lax.ppermute(top, "lat", [(i, (i - 1) % lat) for i in range(lat)])
     low_side = lax.ppermute(side, "lon", [(i, (i + 1) % lon) for i in range(lon)])
     high_side = low_side if lon == 2 else lax.ppermute(
         side, "lon", [(i, (i - 1) % lon) for i in range(lon)])

time: 60.5 us -> 56.9 us (0.940)
  starting transfers between devices: 17.5 us -> 15.7 us
  waiting for transfers between devices: 8.95 us -> 7.26 us
    all_to_all x2, starting transfers between devices: 13.5 us -> 9.87 us  [local(): lax.all_to_all(send, ('lat', 'lon'), split_axis=0, concat_axis=0, tiled=T...]
    ppermute x2, starting transfers between devices: 3.64 us -> 5.69 us  [the longest x1 3.87 us: local(): high = lax.ppermute(top, 'lat', [(i, (i - 1) % lat) for i in range(lat)])]
    all_to_all x2, waiting for transfers between devices: 7.89 us -> 6.07 us  [local(): lax.all_to_all(send, ('lat', 'lon'), split_axis=0, concat_axis=0, tiled=T...]
  transfers between devices with their start and end apart: 5 -> 5, of which waited for: 3 -> 2; matrix products, arithmetic and copies ran while one was open for 0% -> 0% of each run, Pallas kernels for 9% -> 20%
where the time goes in v5:
time: 56.9 us; the launch traced here: 56.7 us
  Pallas kernels  32.9 us (58%)
  starting transfers between devices  15.7 us (28%)
  waiting for transfers between devices  7.26 us (13%)
  between operations  0.76 us (1%)
    pallas_call x1, Pallas kernels, local(): step_kernel(rows, cols, width, lat, waves, lane_rows)  15.1 us
    all_to_all x2, starting transfers between devices, local(): lax.all_to_all(send, ('lat', 'lon'), split_axis=0, concat_axis=0, tiled=T...  9.87 us
    pallas_call x1, Pallas kernels, local(): edge_kernel(rows, cols, width, lat, lon, waves, lane_rows)  6.61 us
    all_to_all x2, waiting for transfers between devices, local(): lax.all_to_all(send, ('lat', 'lon'), split_axis=0, concat_axis=0, tiled=T...  6.07 us
    pallas_call x1, Pallas kernels, local(): synthesis_kernel(bands, rows, lane_rows, steps, lat, lon)  5.75 us
    pallas_call x1, Pallas kernels, local(): values = legendre_kernel(bands, rows, lane_rows, steps)(*place, wavenumbers)  5.49 us
    ppermute x1, starting transfers between devices, local(): high = lax.ppermute(top, 'lat', [(i, (i - 1) % lat) for i in range(lat)])  3.87 us
    ppermute x1, starting transfers between devices, local(): low = lax.ppermute(bottom, 'lat', [(i, (i + 1) % lat) for i in range(lat)])  1.82 us
  transfers between devices with their start and end apart: 5, of which 2 were waited for; matrix products, arithmetic and copies ran while one was open for 0% of the time, Pallas kernels for 20%

profile of v5, /device:TPU:0, one launch (start us, length us, event | category | flops | bytes accessed | tf_op | source)
XLA Modules:
  0.0 56.7 jit_solution(15748606621141493013)
XLA Ops:
  0.6 0.0 copy-start.2
  0.6 6.6 %edge_fourier.1 = (f32[32,2,256]{2,1,0:T(2,128)}, f32[8,4320]{1,0:T(8,128)}, f32[8,4320]{1,0:T(8,128)}, f32[192,128]{1,0:T(8,128)}, bf16[96,4480]{1,0:T(8,128)(2,1)}) custom-call(s32[1]{0:T(128)} %bitcast.band_ref, s32[1]{0:T(128)} %bitcast.1.sector_ref, s32[16]{0:T(128)} %waves_ref.5, f32[1,192,4320]{2,1,0:T(8,128)} %elev.3, f32[1,2,192,4320]{3,2,1,0:T(8,128)} %vel.3, ...), custom_call_target="tpu_custom_call" | custom-call | tf_op jit(solution)/shard_map/edge_fourier/pallas_call | solution.py:644
  7.3 0.0 copy-start.4
  7.3 0.0 copy-start.1
  7.3 7.3 %all-to-all-start = ((f32[32,2,256]{2,1,0:T(2,128)}), f32[32,2,256]{2,1,0:T(2,128)S(1)}, u32[]{:S(2)}, u32[]{:S(2)}) async-start(f32[32,2,256]{2,1,0:T(2,128)} %get-tuple-element.13), calls=%async_computation | async-start | bytes 131072 | tf_op jit(solution)/shard_map/all_to_all | solution.py:646
  14.6 0.0 copy-done.2
  14.6 5.5 %legendre_values.1.values_in = f32[544,8,256]{2,1,0:T(8,128)} custom-call(s32[1]{0:T(128)} %bitcast.band_ref, s32[1]{0:T(128)} %bitcast.1.sector_ref, s32[16]{0:T(128)S(1)} %copy-done.2), custom_call_target="tpu_custom_call" | custom-call | flops 13369344 | bytes 4456448 | tf_op jit(solution)/shard_map/legendre_values/pallas_call | solution.py:647
  20.1 0.0 copy-start.3
  20.1 0.0 copy-start.5
  20.1 0.0 copy-start
  20.2 0.0 copy-done.4
  20.2 1.8 %collective-permute-start = (f32[8,4320]{1,0:T(8,128)S(1)}, f32[8,4320]{1,0:T(8,128)S(1)}, u32[]{:S(2)}, u32[]{:S(2)}) collective-permute-start(f32[8,4320]{1,0:T(8,128)S(1)} %copy-done.4), channel_id=1, source_target_pairs={{0,2},{2,4},{4,6},{6,8},{8,10},{10,12},{12,14},{14,16},{16,18},{18... | collective-permute-start | bytes 414728 | tf_op jit(solution)/shard_map/ppermute | solution.py:649
  22.0 0.0 all-to-all-done.got
  22.0 0.0 copy-done.1
  22.0 5.7 %degree_sums.1 = f32[32,2,256]{2,1,0:T(2,128)} custom-call(s32[1]{0:T(128)} %bitcast.band_ref, s32[1]{0:T(128)} %bitcast.1.sector_ref, s32[16]{0:T(128)S(1)} %copy-done.2, f32[1081]{0:T(1024)S(1)} %copy-done.1, f32[32,2,256]{2,1,0:T(2,128)S(1)} %all-to-all-done.got, f32[544,8,256]{2,1,0:T(8,128)} %legendre_values.1.values_in), custom_call_target="tpu_custom_call" | custom-call | tf_op jit(solution)/shard_map/degree_sums/pallas_call | solution.py:650
  27.8 0.0 copy-done.3
  27.8 3.9 %collective-permute-start.1 = (f32[8,4320]{1,0:T(8,128)S(1)}, f32[8,4320]{1,0:T(8,128)S(1)}, u32[]{:S(2)}, u32[]{:S(2)}) collective-permute-start(f32[8,4320]{1,0:T(8,128)S(1)} %copy-done.3), channel_id=1, source_target_pairs={{0,30},{2,0},{4,2},{6,4},{8,6},{10,8},{12,10},{14,12},{16,14},{18,... | collective-permute-start | bytes 414728 | tf_op jit(solution)/shard_map/ppermute | solution.py:654
  31.7 2.5 %all-to-all-start.1 = ((f32[32,2,256]{2,1,0:T(2,128)}), f32[32,2,256]{2,1,0:T(2,128)S(1)}, u32[]{:S(2)}, u32[]{:S(2)}) async-start(f32[32,2,256]{2,1,0:T(2,128)} %degree_sums.1), calls=%async_computation.1 | async-start | bytes 131072 | tf_op jit(solution)/shard_map/all_to_all | solution.py:653
  34.2 0.0 copy-done.5
  34.2 0.2 collective-permute-start.2
  34.4 0.0 collective-permute-done.low
  34.4 1.2 %collective-permute-done.2.low_side.high_side = f32[192,128]{1,0:T(8,128)S(1)} collective-permute-done((f32[192,128]{1,0:T(8,128)S(1)}, f32[192,128]{1,0:T(8,128)S(1)}, u32[]{:S(2)}, u32[]{:S(2)}) %collective-permute-start.2) | collective-permute-done | bytes 98336 | tf_op jit(solution)/shard_map/ppermute | solution.py:655
  35.6 6.0 %all-to-all-done.1 = f32[32,2,256]{2,1,0:T(2,128)S(1)} async-done(((f32[32,2,256]{2,1,0:T(2,128)}), f32[32,2,256]{2,1,0:T(2,128)S(1)}, u32[]{:S(2)}, u32[]{:S(2)}) %all-to-all-start.1) | async-done | bytes 65568 | tf_op jit(solution)/shard_map/all_to_all | solution.py:653
  41.6 0.0 collective-permute-done.1.high
  41.6 0.0 copy-done
  41.6 15.1 %surge_step.1 = (f32[1,192,4320]{2,1,0:T(8,128)}, f32[1,2,192,4320]{3,2,1,0:T(8,128)}, f32[1,192,4320]{2,1,0:T(8,128)}) custom-call(s32[1]{0:T(128)} %bitcast.band_ref, s32[1]{0:T(128)} %bitcast.1.sector_ref, f32[16,2,2,256]{3,2,1,0:T(2,128)S(1)} %bitcast.3, bf16[96,4480]{1,0:T(8,128)(2,1)S(1)} %copy-done, f32[8,4320]{1,0:T(8,128)S(1)} %collective-permute-done.low, ...), custom_call_target="tpu_custom_call" | custom-call | tf_op jit(solution)/shard_map/surge_step/pallas_call | solution.py:659
Async XLA Ops:
  0.6 14.0 %copy-start.2 = (s32[16]{0:T(128)S(1)}, s32[16]{0:T(128)}, u32[]{:S(2)}) copy-start(s32[16]{0:T(128)} %waves_ref.5) | copy-start | bytes 196
  7.3 12.9 %copy-start.4 = (f32[8,4320]{1,0:T(8,128)S(1)}, f32[8,4320]{1,0:T(8,128)}, u32[]{:S(2)}) copy-start(f32[8,4320]{1,0:T(8,128)} %get-tuple-element.20) | copy-start | bytes 414724
  7.3 14.8 %copy-start.1 = (f32[1081]{0:T(1024)S(1)}, f32[1081]{0:T(1024)}, u32[]{:S(2)}) copy-start(f32[1081]{0:T(1024)} %love.1) | copy-start | bytes 12976
  7.3 14.7 %all-to-all-start = ((f32[32,2,256]{2,1,0:T(2,128)}), f32[32,2,256]{2,1,0:T(2,128)S(1)}, u32[]{:S(2)}, u32[]{:S(2)}) async-start(f32[32,2,256]{2,1,0:T(2,128)} %get-tuple-element.13), calls=%async_computation | async-start | bytes 131072 | tf_op jit(solution)/shard_map/all_to_all | solution.py:646
  20.1 7.7 %copy-start.3 = (f32[8,4320]{1,0:T(8,128)S(1)}, f32[8,4320]{1,0:T(8,128)}, u32[]{:S(2)}) copy-start(f32[8,4320]{1,0:T(8,128)} %get-tuple-element.21) | copy-start | bytes 414724
  20.1 14.1 %copy-start.5 = (f32[192,128]{1,0:T(8,128)S(1)}, f32[192,128]{1,0:T(8,128)}, u32[]{:S(2)}) copy-start(f32[192,128]{1,0:T(8,128)} %get-tuple-element.22) | copy-start | bytes 294916
  20.1 21.5 %copy-start = (bf16[96,4480]{1,0:T(8,128)(2,1)S(1)}, bf16[96,4480]{1,0:T(8,128)(2,1)}, u32[]{:S(2)}) copy-start(bf16[96,4480]{1,0:T(8,128)(2,1)} %get-tuple-element.19.table) | copy-start | bytes 2580484
  20.2 14.2 %collective-permute-start = (f32[8,4320]{1,0:T(8,128)S(1)}, f32[8,4320]{1,0:T(8,128)S(1)}, u32[]{:S(2)}, u32[]{:S(2)}) collective-permute-start(f32[8,4320]{1,0:T(8,128)S(1)} %copy-done.4), channel_id=1, source_target_pairs={{0,2},{2,4},{4,6},{6,8},{8,10},{10,12},{12,14},{14,16},{16,18},{18... | collective-permute-start | bytes 414728 | tf_op jit(solution)/shard_map/ppermute | solution.py:649
  27.8 13.8 %collective-permute-start.1 = (f32[8,4320]{1,0:T(8,128)S(1)}, f32[8,4320]{1,0:T(8,128)S(1)}, u32[]{:S(2)}, u32[]{:S(2)}) collective-permute-start(f32[8,4320]{1,0:T(8,128)S(1)} %copy-done.3), channel_id=1, source_target_pairs={{0,30},{2,0},{4,2},{6,4},{8,6},{10,8},{12,10},{14,12},{16,14},{18,... | collective-permute-start | bytes 414728 | tf_op jit(solution)/shard_map/ppermute | solution.py:654
  31.7 10.0 %all-to-all-start.1 = ((f32[32,2,256]{2,1,0:T(2,128)}), f32[32,2,256]{2,1,0:T(2,128)S(1)}, u32[]{:S(2)}, u32[]{:S(2)}) async-start(f32[32,2,256]{2,1,0:T(2,128)} %degree_sums.1), calls=%async_computation.1 | async-start | bytes 131072 | tf_op jit(solution)/shard_map/all_to_all | solution.py:653
  34.2 1.4 %collective-permute-start.2 = (f32[192,128]{1,0:T(8,128)S(1)}, f32[192,128]{1,0:T(8,128)S(1)}, u32[]{:S(2)}, u32[]{:S(2)}) collective-permute-start(f32[192,128]{1,0:T(8,128)S(1)} %copy-done.5), channel_id=1, source_target_pairs={{0,1},{1,0},{2,3},{3,2},{4,5},{5,4},{6,7},{7,6},{8,9},{9,8},{10,11... | collective-permute-start | bytes 294920 | tf_op jit(solution)/shard_map/ppermute | solution.py:655

commit v6 on v5

--- a/solution.py
+++ b/solution.py
@@ -444,7 +444,9 @@
         elev_v[top + rows : top + rows + 2, :] = high[0:2, :]
         for n, buffer in enumerate((u_v, v_v, wy_v, depth_v, wet_v)):
             buffer[top - 1 : top, :] = low[2 + n : 3 + n, :].astype(buffer.dtype)
-            buffer[top + rows : top + rows + 1, :] = high[2 + n : 3 + n, :].astype(buffer.dtype)
+            behind = high[2 + n : 3 + n, :]
+            behind = jnp.maximum(behind, 0.2) if buffer is depth_v else behind
+            buffer[top + rows : top + rows + 1, :] = behind.astype(buffer.dtype)
 
         group = 4
         after = slice(top + rows, top + rows + 2)
@@ -651,7 +653,7 @@
         *place, wavenumbers, love_factor, got, pltpu.with_memory_space_constraint(values, pltpu.HBM))
     send, top, side = lax.optimization_barrier((send, top, side))
     got = lax.all_to_all(send, ("lat", "lon"), split_axis=0, concat_axis=0, tiled=True)
-    high = lax.ppermute(top, "lat", [(i, (i - 1) % lat) for i in range(lat)])
+    high = lax.ppermute(top, "lat", [(i + 1, i) for i in range(lat - 1)])
     low_side = lax.ppermute(side, "lon", [(i, (i + 1) % lon) for i in range(lon)])
     high_side = low_side if lon == 2 else lax.ppermute(
         side, "lon", [(i, (i - 1) % lon) for i in range(lon)])

time: 56.9 us -> 58.5 us (1.028)
  starting transfers between devices: 15.7 us -> 17.4 us
    all_to_all x2, starting transfers between devices: 9.87 us -> 14 us  [local(): lax.all_to_all(send, ('lat', 'lon'), split_axis=0, concat_axis=0, tiled=T...]
    ppermute x1, starting transfers between devices: 3.87 us -> 1.29 us  [local(): high = lax.ppermute(top, 'lat', [(i + 1, i) for i in range(lat - 1)])]
  transfers between devices with their start and end apart: 5 -> 5, of which waited for: 2 -> 2; matrix products, arithmetic and copies ran while one was open for 0% -> 0% of each run, Pallas kernels for 20% -> 19%
where the time goes in v6:
time: 58.5 us; the launch traced here: 58.3 us
  Pallas kernels  32.9 us (56%)
  starting transfers between devices  17.4 us (30%)
  waiting for transfers between devices  7.12 us (12%)
  between operations  0.77 us (1%)
    pallas_call x1, Pallas kernels, local(): step_kernel(rows, cols, width, lat, waves, lane_rows)  15.1 us
    all_to_all x2, starting transfers between devices, local(): lax.all_to_all(send, ('lat', 'lon'), split_axis=0, concat_axis=0, tiled=T...  14 us
    pallas_call x1, Pallas kernels, local(): edge_kernel(rows, cols, width, lat, lon, waves, lane_rows)  6.61 us
    all_to_all x2, waiting for transfers between devices, local(): lax.all_to_all(send, ('lat', 'lon'), split_axis=0, concat_axis=0, tiled=T...  6.07 us
    pallas_call x1, Pallas kernels, local(): synthesis_kernel(bands, rows, lane_rows, steps, lat, lon)  5.75 us
    pallas_call x1, Pallas kernels, local(): values = legendre_kernel(bands, rows, lane_rows, steps)(*place, wavenumbers)  5.49 us
    ppermute x1, starting transfers between devices, local(): low = lax.ppermute(bottom, 'lat', [(i, (i + 1) % lat) for i in range(lat)])  1.82 us
    ppermute x1, starting transfers between devices, local(): high = lax.ppermute(top, 'lat', [(i + 1, i) for i in range(lat - 1)])  1.29 us
  transfers between devices with their start and end apart: 5, of which 2 were waited for; matrix products, arithmetic and copies ran while one was open for 0% of the time, Pallas kernels for 19%

profile of v6, /device:TPU:0, one launch (start us, length us, event | category | flops | bytes accessed | tf_op | source)
XLA Modules:
  0.0 58.3 jit_solution(18198545327868914890)
XLA Ops:
  0.6 0.0 copy-start.2
  0.6 6.6 %edge_fourier.1 = (f32[32,2,256]{2,1,0:T(2,128)}, f32[8,4320]{1,0:T(8,128)}, f32[8,4320]{1,0:T(8,128)}, f32[192,128]{1,0:T(8,128)}, bf16[96,4480]{1,0:T(8,128)(2,1)}) custom-call(s32[1]{0:T(128)} %bitcast.band_ref, s32[1]{0:T(128)} %bitcast.1.sector_ref, s32[16]{0:T(128)} %waves_ref.5, f32[1,192,4320]{2,1,0:T(8,128)} %elev.3, f32[1,2,192,4320]{3,2,1,0:T(8,128)} %vel.3, ...), custom_call_target="tpu_custom_call" | custom-call | tf_op jit(solution)/shard_map/edge_fourier/pallas_call | solution.py:646
  7.3 0.0 copy-start.4
  7.3 0.0 copy-start.1
  7.3 7.3 %all-to-all-start = ((f32[32,2,256]{2,1,0:T(2,128)}), f32[32,2,256]{2,1,0:T(2,128)S(1)}, u32[]{:S(2)}, u32[]{:S(2)}) async-start(f32[32,2,256]{2,1,0:T(2,128)} %get-tuple-element.13), calls=%async_computation | async-start | bytes 131072 | tf_op jit(solution)/shard_map/all_to_all | solution.py:648
  14.6 0.0 copy-done.2
  14.6 5.5 %legendre_values.1.values_in = f32[544,8,256]{2,1,0:T(8,128)} custom-call(s32[1]{0:T(128)} %bitcast.band_ref, s32[1]{0:T(128)} %bitcast.1.sector_ref, s32[16]{0:T(128)S(1)} %copy-done.2), custom_call_target="tpu_custom_call" | custom-call | flops 13369344 | bytes 4456448 | tf_op jit(solution)/shard_map/legendre_values/pallas_call | solution.py:649
  20.1 0.0 copy-start.3
  20.1 0.0 copy-start.5
  20.1 0.0 copy-start
  20.2 0.0 copy-done.4
  20.2 1.8 %collective-permute-start = (f32[8,4320]{1,0:T(8,128)S(1)}, f32[8,4320]{1,0:T(8,128)S(1)}, u32[]{:S(2)}, u32[]{:S(2)}) collective-permute-start(f32[8,4320]{1,0:T(8,128)S(1)} %copy-done.4), channel_id=1, source_target_pairs={{0,2},{2,4},{4,6},{6,8},{8,10},{10,12},{12,14},{14,16},{16,18},{18... | collective-permute-start | bytes 414728 | tf_op jit(solution)/shard_map/ppermute | solution.py:651
  22.0 0.0 all-to-all-done.got
  22.0 0.0 copy-done.1
  22.0 5.7 %degree_sums.1 = f32[32,2,256]{2,1,0:T(2,128)} custom-call(s32[1]{0:T(128)} %bitcast.band_ref, s32[1]{0:T(128)} %bitcast.1.sector_ref, s32[16]{0:T(128)S(1)} %copy-done.2, f32[1081]{0:T(1024)S(1)} %copy-done.1, f32[32,2,256]{2,1,0:T(2,128)S(1)} %all-to-all-done.got, f32[544,8,256]{2,1,0:T(8,128)} %legendre_values.1.values_in), custom_call_target="tpu_custom_call" | custom-call | tf_op jit(solution)/shard_map/degree_sums/pallas_call | solution.py:652
  27.8 0.0 copy-done.3
  27.8 1.3 %collective-permute-start.1 = (f32[8,4320]{1,0:T(8,128)S(1)}, f32[8,4320]{1,0:T(8,128)S(1)}, u32[]{:S(2)}, u32[]{:S(2)}) collective-permute-start(f32[8,4320]{1,0:T(8,128)S(1)} %copy-done.3), channel_id=1, source_target_pairs={{2,0},{4,2},{6,4},{8,6},{10,8},{12,10},{14,12},{16,14},{18,16},{20... | collective-permute-start | bytes 414728 | tf_op jit(solution)/shard_map/ppermute | solution.py:656
  29.1 6.7 %all-to-all-start.1 = ((f32[32,2,256]{2,1,0:T(2,128)}), f32[32,2,256]{2,1,0:T(2,128)S(1)}, u32[]{:S(2)}, u32[]{:S(2)}) async-start(f32[32,2,256]{2,1,0:T(2,128)} %degree_sums.1), calls=%async_computation.1 | async-start | bytes 131072 | tf_op jit(solution)/shard_map/all_to_all | solution.py:655
  35.8 0.0 copy-done.5
  35.8 0.3 collective-permute-start.2
  36.1 0.0 collective-permute-done.low
  36.1 1.0 %collective-permute-done.2.low_side.high_side = f32[192,128]{1,0:T(8,128)S(1)} collective-permute-done((f32[192,128]{1,0:T(8,128)S(1)}, f32[192,128]{1,0:T(8,128)S(1)}, u32[]{:S(2)}, u32[]{:S(2)}) %collective-permute-start.2) | collective-permute-done | bytes 98336 | tf_op jit(solution)/shard_map/ppermute | solution.py:657
  37.2 6.0 %all-to-all-done.1 = f32[32,2,256]{2,1,0:T(2,128)S(1)} async-done(((f32[32,2,256]{2,1,0:T(2,128)}), f32[32,2,256]{2,1,0:T(2,128)S(1)}, u32[]{:S(2)}, u32[]{:S(2)}) %all-to-all-start.1) | async-done | bytes 65568 | tf_op jit(solution)/shard_map/all_to_all | solution.py:655
  43.2 0.0 collective-permute-done.1.high
  43.2 0.0 copy-done
  43.2 15.1 %surge_step.1 = (f32[1,192,4320]{2,1,0:T(8,128)}, f32[1,2,192,4320]{3,2,1,0:T(8,128)}, f32[1,192,4320]{2,1,0:T(8,128)}) custom-call(s32[1]{0:T(128)} %bitcast.band_ref, s32[1]{0:T(128)} %bitcast.1.sector_ref, f32[16,2,2,256]{3,2,1,0:T(2,128)S(1)} %bitcast.3, bf16[96,4480]{1,0:T(8,128)(2,1)S(1)} %copy-done, f32[8,4320]{1,0:T(8,128)S(1)} %collective-permute-done.low, ...), custom_call_target="tpu_custom_call" | custom-call | tf_op jit(solution)/shard_map/surge_step/pallas_call | solution.py:661
Async XLA Ops:
  0.6 14.0 %copy-start.2 = (s32[16]{0:T(128)S(1)}, s32[16]{0:T(128)}, u32[]{:S(2)}) copy-start(s32[16]{0:T(128)} %waves_ref.5) | copy-start | bytes 196
  7.3 12.9 %copy-start.4 = (f32[8,4320]{1,0:T(8,128)S(1)}, f32[8,4320]{1,0:T(8,128)}, u32[]{:S(2)}) copy-start(f32[8,4320]{1,0:T(8,128)} %get-tuple-element.20) | copy-start | bytes 414724
  7.3 14.8 %copy-start.1 = (f32[1081]{0:T(1024)S(1)}, f32[1081]{0:T(1024)}, u32[]{:S(2)}) copy-start(f32[1081]{0:T(1024)} %love.1) | copy-start | bytes 12976
  7.3 14.7 %all-to-all-start = ((f32[32,2,256]{2,1,0:T(2,128)}), f32[32,2,256]{2,1,0:T(2,128)S(1)}, u32[]{:S(2)}, u32[]{:S(2)}) async-start(f32[32,2,256]{2,1,0:T(2,128)} %get-tuple-element.13), calls=%async_computation | async-start | bytes 131072 | tf_op jit(solution)/shard_map/all_to_all | solution.py:648
  20.1 7.7 %copy-start.3 = (f32[8,4320]{1,0:T(8,128)S(1)}, f32[8,4320]{1,0:T(8,128)}, u32[]{:S(2)}) copy-start(f32[8,4320]{1,0:T(8,128)} %get-tuple-element.21) | copy-start | bytes 414724
  20.1 15.7 %copy-start.5 = (f32[192,128]{1,0:T(8,128)S(1)}, f32[192,128]{1,0:T(8,128)}, u32[]{:S(2)}) copy-start(f32[192,128]{1,0:T(8,128)} %get-tuple-element.22) | copy-start | bytes 294916
  20.1 23.1 %copy-start = (bf16[96,4480]{1,0:T(8,128)(2,1)S(1)}, bf16[96,4480]{1,0:T(8,128)(2,1)}, u32[]{:S(2)}) copy-start(bf16[96,4480]{1,0:T(8,128)(2,1)} %get-tuple-element.19.table) | copy-start | bytes 2580484
  20.2 15.9 %collective-permute-start = (f32[8,4320]{1,0:T(8,128)S(1)}, f32[8,4320]{1,0:T(8,128)S(1)}, u32[]{:S(2)}, u32[]{:S(2)}) collective-permute-start(f32[8,4320]{1,0:T(8,128)S(1)} %copy-done.4), channel_id=1, source_target_pairs={{0,2},{2,4},{4,6},{6,8},{8,10},{10,12},{12,14},{14,16},{16,18},{18... | collective-permute-start | bytes 414728 | tf_op jit(solution)/shard_map/ppermute | solution.py:651
  27.8 15.4 %collective-permute-start.1 = (f32[8,4320]{1,0:T(8,128)S(1)}, f32[8,4320]{1,0:T(8,128)S(1)}, u32[]{:S(2)}, u32[]{:S(2)}) collective-permute-start(f32[8,4320]{1,0:T(8,128)S(1)} %copy-done.3), channel_id=1, source_target_pairs={{2,0},{4,2},{6,4},{8,6},{10,8},{12,10},{14,12},{16,14},{18,16},{20... | collective-permute-start | bytes 414728 | tf_op jit(solution)/shard_map/ppermute | solution.py:656
  29.1 14.1 %all-to-all-start.1 = ((f32[32,2,256]{2,1,0:T(2,128)}), f32[32,2,256]{2,1,0:T(2,128)S(1)}, u32[]{:S(2)}, u32[]{:S(2)}) async-start(f32[32,2,256]{2,1,0:T(2,128)} %degree_sums.1), calls=%async_computation.1 | async-start | bytes 131072 | tf_op jit(solution)/shard_map/all_to_all | solution.py:655
  35.8 1.4 %collective-permute-start.2 = (f32[192,128]{1,0:T(8,128)S(1)}, f32[192,128]{1,0:T(8,128)S(1)}, u32[]{:S(2)}, u32[]{:S(2)}) collective-permute-start(f32[192,128]{1,0:T(8,128)S(1)} %copy-done.5), channel_id=1, source_target_pairs={{0,1},{1,0},{2,3},{3,2},{4,5},{5,4},{6,7},{7,6},{8,9},{9,8},{10,11... | collective-permute-start | bytes 294920 | tf_op jit(solution)/shard_map/ppermute | solution.py:657

commit v7 on v6

--- a/solution.py
+++ b/solution.py
@@ -125,15 +125,12 @@
 
         for copy in copies:
             copy.wait()
-        top[0:2, :] = elev_v[0:2, :]
-        bottom[0:2, :] = elev_v[rows - 2 : rows, :]
-        for n in range(4):
-            top[2 + n : 3 + n, :] = top_v[n]
-            bottom[2 + n : 3 + n, :] = bottom_v[n]
-        top[6:7, :] = wet_v[0:1, :].astype(f32)
-        bottom[6:7, :] = wet_v[rows - 1 : rows, :].astype(f32)
-        top[7:8, :] = jnp.zeros((1, cols), f32)
-        bottom[7:8, :] = jnp.zeros((1, cols), f32)
+        for which, edge, start, line in ((top, top_v, 0, 0), (bottom, bottom_v, rows - 2, rows - 1)):
+            u, v, wind_y, d = (edge[n] for n in range(4))
+            drag = wet_v[line : line + 1, :].astype(f32) / (d + 0.1 * jnp.sqrt(u * u + v * v))
+            which[0:2, :] = elev_v[start : start + 2, :]
+            which[2:3, :] = d * drag * (wind_y + d * v)
+            which[3:4, :] = d * d * drag
         blank = jnp.zeros((8, LANES - tail), f32)
         for start in range(0, rows, 8):
             here = slice(start, start + 8)
@@ -155,8 +152,8 @@
         body,
         out_shape=(
             jax.ShapeDtypeStruct((lat * lon, 2, lane_rows), f32),
-            jax.ShapeDtypeStruct((8, cols), f32),
-            jax.ShapeDtypeStruct((8, cols), f32),
+            jax.ShapeDtypeStruct((4, cols), f32),
+            jax.ShapeDtypeStruct((4, cols), f32),
             jax.ShapeDtypeStruct((rows, LANES), f32),
             jax.ShapeDtypeStruct((6 * waves, width), bf16),
         ),
@@ -442,11 +439,14 @@
 
         elev_v[top - 2 : top, :] = low[0:2, :]
         elev_v[top + rows : top + rows + 2, :] = high[0:2, :]
-        for n, buffer in enumerate((u_v, v_v, wy_v, depth_v, wet_v)):
-            buffer[top - 1 : top, :] = low[2 + n : 3 + n, :].astype(buffer.dtype)
-            behind = high[2 + n : 3 + n, :]
-            behind = jnp.maximum(behind, 0.2) if buffer is depth_v else behind
-            buffer[top + rows : top + rows + 1, :] = behind.astype(buffer.dtype)
+        for line, block in ((top - 1, low), (top + rows, high)):
+            push, give = block[2:3, :], block[3:4, :]
+            spot = slice(line, line + 1)
+            u_v[spot, :] = jnp.zeros((1, cols), f32)
+            v_v[spot, :] = jnp.zeros((1, cols), f32)
+            wy_v[spot, :] = push
+            depth_v[spot, :] = jnp.where(give > 0.0, give, 1.0)
+            wet_v[spot, :] = jnp.where(give > 0.0, 1, 0)
 
         group = 4
         after = slice(top + rows, top + rows + 2)

time: 58.5 us -> 56.2 us (0.961)
  starting transfers between devices: 17.4 us -> 14.6 us
    ppermute x1, waiting for transfers between devices: 0.01 us -> 5.83 us  [local(): low = lax.ppermute(bottom, 'lat', [(i, (i + 1) % lat) for i in range(lat)])]
    all_to_all x2, waiting for transfers between devices: 6.07 us -> 1.86 us  [local(): lax.all_to_all(send, ('lat', 'lon'), split_axis=0, concat_axis=0, tiled=T...]
    all_to_all x2, starting transfers between devices: 14 us -> 11.3 us  [local(): lax.all_to_all(send, ('lat', 'lon'), split_axis=0, concat_axis=0, tiled=T...]
    ppermute x1, waiting for transfers between devices: 1.05 us -> 0.01 us  [local(): lax.ppermute(side, 'lon', [(i, (i + 1) % lon) for i in range(lon)])]
  transfers between devices with their start and end apart: 5 -> 5, of which waited for: 2 -> 2; matrix products, arithmetic and copies ran while one was open for 0% -> 0% of each run, Pallas kernels for 19% -> 10%
where the time goes in v7:
time: 56.2 us; the launch traced here: 55.9 us
  Pallas kernels  32.9 us (59%)
  starting transfers between devices  14.6 us (26%)
  waiting for transfers between devices  7.69 us (14%)
  between operations  0.76 us (1%)
    pallas_call x1, Pallas kernels, local(): step_kernel(rows, cols, width, lat, waves, lane_rows)  15.1 us
    all_to_all x2, starting transfers between devices, local(): lax.all_to_all(send, ('lat', 'lon'), split_axis=0, concat_axis=0, tiled=T...  11.3 us
    pallas_call x1, Pallas kernels, local(): edge_kernel(rows, cols, width, lat, lon, waves, lane_rows)  6.57 us
    ppermute x1, waiting for transfers between devices, local(): low = lax.ppermute(bottom, 'lat', [(i, (i + 1) % lat) for i in range(lat)])  5.83 us
    pallas_call x1, Pallas kernels, local(): synthesis_kernel(bands, rows, lane_rows, steps, lat, lon)  5.74 us
    pallas_call x1, Pallas kernels, local(): values = legendre_kernel(bands, rows, lane_rows, steps)(*place, wavenumbers)  5.49 us
    all_to_all x2, waiting for transfers between devices, local(): lax.all_to_all(send, ('lat', 'lon'), split_axis=0, concat_axis=0, tiled=T...  1.86 us
    ppermute x1, starting transfers between devices, local(): low = lax.ppermute(bottom, 'lat', [(i, (i + 1) % lat) for i in range(lat)])  1.63 us
  transfers between devices with their start and end apart: 5, of which 2 were waited for; matrix products, arithmetic and copies ran while one was open for 0% of the time, Pallas kernels for 10%

profile of v7, /device:TPU:0, one launch (start us, length us, event | category | flops | bytes accessed | tf_op | source)
XLA Modules:
  0.0 55.9 jit_solution(7782855795777599236)
XLA Ops:
  0.6 0.0 copy-start.2
  0.6 6.6 %edge_fourier.1 = (f32[32,2,256]{2,1,0:T(2,128)}, f32[4,4320]{1,0:T(4,128)}, f32[4,4320]{1,0:T(4,128)}, f32[192,128]{1,0:T(8,128)}, bf16[96,4480]{1,0:T(8,128)(2,1)}) custom-call(s32[1]{0:T(128)} %bitcast.band_ref, s32[1]{0:T(128)} %bitcast.1.sector_ref, s32[16]{0:T(128)} %waves_ref.5, f32[1,192,4320]{2,1,0:T(8,128)} %elev.3, f32[1,2,192,4320]{3,2,1,0:T(8,128)} %vel.3, ...), custom_call_target="tpu_custom_call" | custom-call | tf_op jit(solution)/shard_map/edge_fourier/pallas_call | solution.py:646
  7.2 0.0 copy-start.1
  7.2 7.3 %all-to-all-start = ((f32[32,2,256]{2,1,0:T(2,128)}), f32[32,2,256]{2,1,0:T(2,128)S(1)}, u32[]{:S(2)}, u32[]{:S(2)}) async-start(f32[32,2,256]{2,1,0:T(2,128)} %get-tuple-element.13), calls=%async_computation | async-start | bytes 131072 | tf_op jit(solution)/shard_map/all_to_all | solution.py:648
  14.6 0.0 copy-done.2
  14.6 5.5 %legendre_values.1.values_in = f32[544,8,256]{2,1,0:T(8,128)} custom-call(s32[1]{0:T(128)} %bitcast.band_ref, s32[1]{0:T(128)} %bitcast.1.sector_ref, s32[16]{0:T(128)S(1)} %copy-done.2), custom_call_target="tpu_custom_call" | custom-call | flops 13369344 | bytes 4456448 | tf_op jit(solution)/shard_map/legendre_values/pallas_call | solution.py:649
  20.1 0.0 copy-start.3
  20.1 0.0 copy-start.5
  20.1 0.0 copy-start.4
  20.1 0.0 copy-start
  20.1 1.9 %all-to-all-done.got = f32[32,2,256]{2,1,0:T(2,128)S(1)} async-done(((f32[32,2,256]{2,1,0:T(2,128)}), f32[32,2,256]{2,1,0:T(2,128)S(1)}, u32[]{:S(2)}, u32[]{:S(2)}) %all-to-all-start) | async-done | bytes 65568 | tf_op jit(solution)/shard_map/all_to_all | solution.py:648
  22.0 0.0 copy-done.1
  22.0 5.7 %degree_sums.1 = f32[32,2,256]{2,1,0:T(2,128)} custom-call(s32[1]{0:T(128)} %bitcast.band_ref, s32[1]{0:T(128)} %bitcast.1.sector_ref, s32[16]{0:T(128)S(1)} %copy-done.2, f32[1081]{0:T(1024)S(1)} %copy-done.1, f32[32,2,256]{2,1,0:T(2,128)S(1)} %all-to-all-done.got, f32[544,8,256]{2,1,0:T(8,128)} %legendre_values.1.values_in), custom_call_target="tpu_custom_call" | custom-call | tf_op jit(solution)/shard_map/degree_sums/pallas_call | solution.py:652
  27.7 4.0 %all-to-all-start.1 = ((f32[32,2,256]{2,1,0:T(2,128)}), f32[32,2,256]{2,1,0:T(2,128)S(1)}, u32[]{:S(2)}, u32[]{:S(2)}) async-start(f32[32,2,256]{2,1,0:T(2,128)} %degree_sums.1), calls=%async_computation.1 | async-start | bytes 131072 | tf_op jit(solution)/shard_map/all_to_all | solution.py:655
  31.7 0.0 copy-done.3
  31.8 0.3 collective-permute-start.2
  32.1 0.0 copy-done.5
  32.1 1.6 %collective-permute-start = (f32[4,4320]{1,0:T(4,128)S(1)}, f32[4,4320]{1,0:T(4,128)S(1)}, u32[]{:S(2)}, u32[]{:S(2)}) collective-permute-start(f32[4,4320]{1,0:T(4,128)S(1)} %copy-done.5), channel_id=1, source_target_pairs={{0,2},{2,4},{4,6},{6,8},{8,10},{10,12},{12,14},{14,16},{16,18},{18... | collective-permute-start | bytes 207368 | tf_op jit(solution)/shard_map/ppermute | solution.py:651
  33.7 0.0 copy-done.4
  33.7 1.3 %collective-permute-start.1 = (f32[4,4320]{1,0:T(4,128)S(1)}, f32[4,4320]{1,0:T(4,128)S(1)}, u32[]{:S(2)}, u32[]{:S(2)}) collective-permute-start(f32[4,4320]{1,0:T(4,128)S(1)} %copy-done.4), channel_id=1, source_target_pairs={{2,0},{4,2},{6,4},{8,6},{10,8},{12,10},{14,12},{16,14},{18,16},{20... | collective-permute-start | bytes 207368 | tf_op jit(solution)/shard_map/ppermute | solution.py:656
  35.0 5.8 %collective-permute-done.low = f32[4,4320]{1,0:T(4,128)S(1)} collective-permute-done((f32[4,4320]{1,0:T(4,128)S(1)}, f32[4,4320]{1,0:T(4,128)S(1)}, u32[]{:S(2)}, u32[]{:S(2)}) %collective-permute-start) | collective-permute-done | bytes 69152 | tf_op jit(solution)/shard_map/ppermute | solution.py:651
  40.8 0.0 collective-permute-done.1.high
  40.8 0.0 collective-permute-done.2.low_side.high_side
  40.8 0.0 all-to-all-done.1
  40.8 0.0 copy-done
  40.8 15.1 %surge_step.1 = (f32[1,192,4320]{2,1,0:T(8,128)}, f32[1,2,192,4320]{3,2,1,0:T(8,128)}, f32[1,192,4320]{2,1,0:T(8,128)}) custom-call(s32[1]{0:T(128)} %bitcast.band_ref, s32[1]{0:T(128)} %bitcast.1.sector_ref, f32[16,2,2,256]{3,2,1,0:T(2,128)S(1)} %bitcast.3, bf16[96,4480]{1,0:T(8,128)(2,1)S(1)} %copy-done, f32[4,4320]{1,0:T(4,128)S(1)} %collective-permute-done.low, ...), custom_call_target="tpu_custom_call" | custom-call | tf_op jit(solution)/shard_map/surge_step/pallas_call | solution.py:661
Async XLA Ops:
  0.6 13.9 %copy-start.2 = (s32[16]{0:T(128)S(1)}, s32[16]{0:T(128)}, u32[]{:S(2)}) copy-start(s32[16]{0:T(128)} %waves_ref.5) | copy-start | bytes 196
  7.2 14.8 %copy-start.1 = (f32[1081]{0:T(1024)S(1)}, f32[1081]{0:T(1024)}, u32[]{:S(2)}) copy-start(f32[1081]{0:T(1024)} %love.1) | copy-start | bytes 12976
  7.2 14.7 %all-to-all-start = ((f32[32,2,256]{2,1,0:T(2,128)}), f32[32,2,256]{2,1,0:T(2,128)S(1)}, u32[]{:S(2)}, u32[]{:S(2)}) async-start(f32[32,2,256]{2,1,0:T(2,128)} %get-tuple-element.13), calls=%async_computation | async-start | bytes 131072 | tf_op jit(solution)/shard_map/all_to_all | solution.py:648
  20.1 11.7 %copy-start.3 = (f32[192,128]{1,0:T(8,128)S(1)}, f32[192,128]{1,0:T(8,128)}, u32[]{:S(2)}) copy-start(f32[192,128]{1,0:T(8,128)} %get-tuple-element.22) | copy-start | bytes 294916
  20.1 12.0 %copy-start.5 = (f32[4,4320]{1,0:T(4,128)S(1)}, f32[4,4320]{1,0:T(4,128)}, u32[]{:S(2)}) copy-start(f32[4,4320]{1,0:T(4,128)} %get-tuple-element.20) | copy-start | bytes 207364
  20.1 13.6 %copy-start.4 = (f32[4,4320]{1,0:T(4,128)S(1)}, f32[4,4320]{1,0:T(4,128)}, u32[]{:S(2)}) copy-start(f32[4,4320]{1,0:T(4,128)} %get-tuple-element.21) | copy-start | bytes 207364
  20.1 20.7 %copy-start = (bf16[96,4480]{1,0:T(8,128)(2,1)S(1)}, bf16[96,4480]{1,0:T(8,128)(2,1)}, u32[]{:S(2)}) copy-start(bf16[96,4480]{1,0:T(8,128)(2,1)} %get-tuple-element.19.table) | copy-start | bytes 2580484
  27.7 13.1 %all-to-all-start.1 = ((f32[32,2,256]{2,1,0:T(2,128)}), f32[32,2,256]{2,1,0:T(2,128)S(1)}, u32[]{:S(2)}, u32[]{:S(2)}) async-start(f32[32,2,256]{2,1,0:T(2,128)} %degree_sums.1), calls=%async_computation.1 | async-start | bytes 131072 | tf_op jit(solution)/shard_map/all_to_all | solution.py:655
  31.8 9.1 %collective-permute-start.2 = (f32[192,128]{1,0:T(8,128)S(1)}, f32[192,128]{1,0:T(8,128)S(1)}, u32[]{:S(2)}, u32[]{:S(2)}) collective-permute-start(f32[192,128]{1,0:T(8,128)S(1)} %copy-done.3), channel_id=1, source_target_pairs={{0,1},{1,0},{2,3},{3,2},{4,5},{5,4},{6,7},{7,6},{8,9},{9,8},{10,11... | collective-permute-start | bytes 294920 | tf_op jit(solution)/shard_map/ppermute | solution.py:657
  32.1 8.8 %collective-permute-start = (f32[4,4320]{1,0:T(4,128)S(1)}, f32[4,4320]{1,0:T(4,128)S(1)}, u32[]{:S(2)}, u32[]{:S(2)}) collective-permute-start(f32[4,4320]{1,0:T(4,128)S(1)} %copy-done.5), channel_id=1, source_target_pairs={{0,2},{2,4},{4,6},{6,8},{8,10},{10,12},{12,14},{14,16},{16,18},{18... | collective-permute-start | bytes 207368 | tf_op jit(solution)/shard_map/ppermute | solution.py:651
  33.7 7.1 %collective-permute-start.1 = (f32[4,4320]{1,0:T(4,128)S(1)}, f32[4,4320]{1,0:T(4,128)S(1)}, u32[]{:S(2)}, u32[]{:S(2)}) collective-permute-start(f32[4,4320]{1,0:T(4,128)S(1)} %copy-done.4), channel_id=1, source_target_pairs={{2,0},{4,2},{6,4},{8,6},{10,8},{12,10},{14,12},{16,14},{18,16},{20... | collective-permute-start | bytes 207368 | tf_op jit(solution)/shard_map/ppermute | solution.py:656
